TPU v7x, 32 devices: a whole 2x2x4 slice. The times are simulated.
32 devices in a mesh: section: 4 (over y, x), seq: 8 (over z, core).
Axes of the slice: x: 2, y: 2, z: 4, core: 2. Of those that a mesh axis runs over, the one named last changes fastest.
Arguments:
- tokens: bfloat16 [1024, 1024], P('seq'), may hold values from -6 to 6
- cotangent: bfloat16 [1024, 1024], P('seq'), may hold values from -6 to 6
- norm_gain: float32 [4, 1024], P('section'), may hold values from 0.1 to 1.9
- w_inner: bfloat16 [4, 1024, 2048], P('section'), may hold values from -0.1875 to 0.1875
- w_outer: bfloat16 [4, 1024, 1024], P('section'), may hold values from -0.75 to 0.75
- rpe_periods: int32 [4, 32], P('section'), may hold values from 1 to 511
- rpe_in: float32 [4, 64, 64], P('section'), may hold values from -0.75 to 0.75
- rpe_mid: float32 [4, 64, 64], P('section'), may hold values from -0.75 to 0.75
- rpe_out: float32 [4, 64, 1024], P('section', None, 'seq'), may hold values from -3 to 3
- decay: float32 [4, 1024], P('section', 'seq'), may hold values from 0.00048828125 to 0.03
Outputs:
- section_out: bfloat16 [4, 1024, 1024], P('section', 'seq')
- section_in_grad: bfloat16 [4, 1024, 1024], P('section', 'seq')
- inner_grad: float32 [4, 1024, 2048], P('section', 'seq')
- outer_grad: float32 [4, 1024, 1024], P('section', 'seq')
All inputs are finite; a program needn't handle non-finite values.
Results may differ from a plain program's by a relative error of at most 0.025.
Values may be sent and summed in bfloat16 or wider, within the bound.
A program may use at most 128 MiB of HBM per device.

v0:
```python
import math

import jax
import jax.numpy as jnp
from jax import lax
from jax.sharding import PartitionSpec as P

EPSILON = 1e-06
PRECISE = lax.Precision.HIGHEST


def passed_along(value, axis, steps):
    count = lax.axis_size(axis)
    initial, last = (max(0, -steps), min(count, count - steps))
    return lax.ppermute(value, axis, [(source, source + steps) for source in range(initial, last)])


def kernel_rows(periods, weight_in, weight_mid, weight_out, decay_rate, seq_length):
    positions = jnp.arange(seq_length, dtype=jnp.int32)
    turn_count = periods[:, None] * positions[None, :] % seq_length
    angles = turn_count.astype(jnp.float32) * (2.0 * math.pi / seq_length)
    features = jnp.concatenate([jnp.sin(angles), jnp.cos(angles)], axis=0)
    hidden = jax.nn.relu(jnp.dot(weight_in.T, features, precision=PRECISE))
    hidden = jax.nn.relu(jnp.dot(weight_mid.T, hidden, precision=PRECISE))
    raw_rows = jnp.dot(weight_out.T, hidden, precision=PRECISE)
    place = positions.astype(jnp.float32)
    norm_scale = jnp.sqrt(1.0 - jnp.exp(-2.0 * decay_rate))
    return raw_rows * norm_scale[:, None] * jnp.exp(-decay_rate[:, None] * place[None, :])


def silu_slope(pre_act):
    sigmoid_val = jax.nn.sigmoid(pre_act)
    return sigmoid_val * (1.0 + pre_act * (1.0 - sigmoid_val))


def split_size(fft_size):
    return math.gcd(fft_size, 1 << (fft_size.bit_length() - 1) // 2)


def dft_table(length, sign_value):
    indices = jnp.arange(length, dtype=jnp.int32)
    turn_count = indices[:, None] * indices[None, :] % length
    angles = turn_count.astype(jnp.float32) * (sign_value * 2.0 * math.pi / length)
    return (jnp.cos(angles), jnp.sin(angles))


def twiddle_table(count_rows, count_cols, sign_value):
    fft_size = count_rows * count_cols
    turn_count = (
        jnp.arange(count_rows, dtype=jnp.int32)[:, None]
        * jnp.arange(count_cols, dtype=jnp.int32)[None, :]
    )
    angles = turn_count.astype(jnp.float32) * (sign_value * 2.0 * math.pi / fft_size)
    return (jnp.cos(angles), jnp.sin(angles))


def half_table(size_second):
    half_cols = size_second // 2
    turn_count = (
        jnp.arange(half_cols, dtype=jnp.int32)[:, None]
        * jnp.arange(size_second, dtype=jnp.int32)[None, :]
        % size_second
    )
    angles = turn_count.astype(jnp.float32) * (2.0 * math.pi / size_second)
    return (jnp.cos(angles), jnp.sin(angles))


def parity_signs(size_second):
    return 1.0 - 2.0 * (jnp.arange(size_second, dtype=jnp.int32) % 2).astype(jnp.float32)


def spectrum(signal, size_first):
    own_chans, seq_length = signal.shape
    fft_size = 2 * seq_length
    size_second = fft_size // size_first
    half_rows = size_first // 2
    shaped = signal.reshape(own_chans, half_rows, size_second)
    first_re, first_im = dft_table(size_first, -1.0)
    first_both = jnp.concatenate([first_re[:, :half_rows], first_im[:, :half_rows]], axis=0)
    section = jnp.einsum("kp,cpq->ckq", first_both, shaped, precision=PRECISE)
    section_re = section[:, :size_first]
    section_im = section[:, size_first:]
    twist_re, twist_im = twiddle_table(size_first, size_second, -1.0)
    turned = jnp.concatenate(
        [
            section_re * twist_re - section_im * twist_im,
            section_re * twist_im + section_im * twist_re,
        ],
        axis=2,
    )
    cos_rows, sin_rows = half_table(size_second)
    cos_cols = cos_rows.T
    sin_cols = sin_rows.T
    second_both = jnp.concatenate(
        [
            jnp.concatenate([cos_cols, -sin_cols], axis=1),
            jnp.concatenate([sin_cols, cos_cols], axis=1),
        ],
        axis=0,
    )
    spec = jnp.einsum("ckq,qm->ckm", turned, second_both, precision=PRECISE)
    nyquist = jnp.einsum("cpq,q->c", shaped, parity_signs(size_second), precision=PRECISE)
    return (spec, nyquist[:, None])


def to_signal(spec, nyquist, size_first):
    own_chans, _, size_second = spec.shape
    half_cols = size_second // 2
    half_rows = size_first // 2
    fft_size = size_first * size_second
    row_ids = jnp.arange(size_first, dtype=jnp.int32)[:, None]
    col_ids = jnp.arange(half_cols, dtype=jnp.int32)[None, :]
    weights = jnp.where((row_ids == 0) & (col_ids == 0), 1.0, 2.0).astype(jnp.float32)
    weighted = spec * jnp.concatenate([weights, weights], axis=1)
    cos_rows, sin_rows = half_table(size_second)
    inner_both = jnp.concatenate(
        [
            jnp.concatenate([cos_rows, sin_rows], axis=1),
            jnp.concatenate([-sin_rows, cos_rows], axis=1),
        ],
        axis=0,
    )
    section = jnp.einsum("ckm,mq->ckq", weighted, inner_both, precision=PRECISE)
    section_re = section[:, :, :size_second]
    section_im = section[:, :, size_second:]
    twist_re, twist_im = twiddle_table(size_first, size_second, 1.0)
    turned = jnp.concatenate(
        [
            section_re * twist_re - section_im * twist_im,
            section_re * twist_im + section_im * twist_re,
        ],
        axis=1,
    )
    first_re, first_im = dft_table(size_first, 1.0)
    outer_both = jnp.concatenate([first_re[:half_rows], -first_im[:half_rows]], axis=1)
    signal = jnp.einsum("pk,ckq->cpq", outer_both, turned, precision=PRECISE)
    signal = signal + nyquist[:, :, None] * parity_signs(size_second)[None, None, :]
    return (signal / fft_size).reshape(own_chans, half_rows * size_second)


def on_device(
    tokens, cotangent, norm_gain, w_inner, w_outer, rpe_periods, rpe_in, rpe_mid, rpe_out, decay
):
    tok_rows, model_width = tokens.shape
    seq_parts = lax.axis_size("seq")
    seq_length = tok_rows * seq_parts
    own_chans = model_width // seq_parts
    fft_size = 2 * seq_length
    size_first = split_size(fft_size)
    half_cols = fft_size // size_first // 2
    section_index = lax.axis_index("section")
    section_count = lax.axis_size("section")
    grad_scale = 1.0 / math.sqrt(seq_length)
    gain_row = norm_gain[0]
    inner_weight = w_inner[0]
    outer_weight = w_outer[0]

    def to_channels(block):
        return lax.all_to_all(block, "seq", split_axis=0, concat_axis=1, tiled=True)

    def to_tokens(block):
        return lax.all_to_all(block, "seq", split_axis=1, concat_axis=0, tiled=True)

    def pass_section(block, offset):
        return passed_along(block, "section", offset)

    def token_front(inputs):
        x_float = inputs.astype(jnp.float32)
        inv_rms = lax.rsqrt(jnp.mean(x_float * x_float, axis=1, keepdims=True) + EPSILON)
        normed = (x_float * inv_rms * gain_row[None, :]).astype(jnp.bfloat16)
        pre_act = jnp.einsum("td,de->et", normed, inner_weight, preferred_element_type=jnp.float32)
        value_act = jax.nn.silu(pre_act[model_width:]).astype(jnp.bfloat16)
        return (inv_rms, normed, pre_act, value_act)

    kernel = kernel_rows(rpe_periods[0], rpe_in[0], rpe_mid[0], rpe_out[0], decay[0], seq_length)
    forward_spec, forward_nyq = spectrum(kernel, size_first)

    def channel_forward(value_chan):
        value_spec, value_nyq = spectrum(value_chan.astype(jnp.float32), size_first)
        kernel_re = forward_spec[:, :, :half_cols]
        kernel_im = forward_spec[:, :, half_cols:]
        value_re = value_spec[:, :, :half_cols]
        value_im = value_spec[:, :, half_cols:]
        product = jnp.concatenate(
            [
                value_re * kernel_re - value_im * kernel_im,
                value_re * kernel_im + value_im * kernel_re,
            ],
            axis=2,
        )
        mixed_chan = to_signal(product, value_nyq * forward_nyq, size_first)
        return mixed_chan.astype(jnp.bfloat16)

    def token_back(inputs, pre_act, mixed_tok):
        gate_act = jax.nn.silu(pre_act[:model_width]).astype(jnp.bfloat16)
        gated = (gate_act.astype(jnp.float32) * mixed_tok.astype(jnp.float32)).astype(jnp.bfloat16)
        update = jnp.einsum("et,ef->tf", gated, outer_weight, preferred_element_type=jnp.float32)
        return (gated, (inputs.astype(jnp.float32) + update).astype(jnp.bfloat16))

    zero_tok = jnp.zeros((tok_rows, model_width), jnp.bfloat16)
    zero_cols = jnp.zeros((model_width, tok_rows), jnp.bfloat16)
    zero_chan = jnp.zeros((own_chans, seq_length), jnp.bfloat16)
    current = tokens
    kept_input = zero_tok
    kept_front = (
        jnp.zeros((tok_rows, 1), jnp.float32),
        zero_tok,
        jnp.zeros((2 * model_width, tok_rows), jnp.float32),
        zero_cols,
    )
    kept_mixed = zero_cols
    kept_gated = zero_cols
    produced = zero_tok
    for section_step in range(section_count):
        active = section_index == section_step
        source = current
        kept_input = jnp.where(active, source, kept_input)
        kept_front = lax.cond(
            active, lambda: token_front(source), lambda previous=kept_front: previous
        )
        value_chan = to_channels(kept_front[3])
        mixed_chan = lax.cond(active, lambda: channel_forward(value_chan), lambda: zero_chan)
        mixed_tok = to_tokens(mixed_chan)
        kept_mixed = jnp.where(active, mixed_tok, kept_mixed)
        front_now = kept_front
        kept_gated, produced = lax.cond(
            active,
            lambda: token_back(source, front_now[2], mixed_tok),
            lambda previous=(kept_gated, produced): previous,
        )
        if section_step + 1 < section_count:
            current = pass_section(produced, 1)
    inv_rms, normed, pre_act, value_act = kept_front
    backward_spec, backward_nyq = (forward_spec, forward_nyq)

    def grad_front(grad_out):
        dgated = jnp.einsum("tf,ef->et", grad_out, outer_weight, preferred_element_type=jnp.float32)
        gate_act = jax.nn.silu(pre_act[:model_width]).astype(jnp.bfloat16)
        dmixed = (dgated * gate_act.astype(jnp.float32)).astype(jnp.bfloat16)
        return (dmixed, dgated * kept_mixed.astype(jnp.float32))

    def channel_backward(dmixed_chan):
        kernel_re = backward_spec[:, :, :half_cols]
        kernel_im = backward_spec[:, :, half_cols:]
        grad_spec, grad_nyq = spectrum(dmixed_chan.astype(jnp.float32), size_first)
        grad_re = grad_spec[:, :, :half_cols]
        grad_im = grad_spec[:, :, half_cols:]
        product = jnp.concatenate(
            [grad_re * kernel_re + grad_im * kernel_im, grad_im * kernel_re - grad_re * kernel_im],
            axis=2,
        )
        dvalue_chan = to_signal(product, grad_nyq * backward_nyq, size_first)
        return dvalue_chan.astype(jnp.bfloat16)

    def grad_back(dvalue_tok, dgate, grad_out):
        dpre = jnp.concatenate(
            [
                dgate * silu_slope(pre_act[:model_width]),
                dvalue_tok.astype(jnp.float32) * silu_slope(pre_act[model_width:]),
            ],
            axis=0,
        ).astype(jnp.bfloat16)
        dnormed = jnp.einsum("et,de->td", dpre, inner_weight, preferred_element_type=jnp.float32)
        x_float = kept_input.astype(jnp.float32)
        dscaled = dnormed * gain_row[None, :]
        x_hat = x_float * inv_rms
        shared = jnp.mean(dscaled * x_hat, axis=1, keepdims=True)
        grad_in = (grad_out.astype(jnp.float32) + inv_rms * (dscaled - x_hat * shared)).astype(
            jnp.bfloat16
        )
        return (dpre, grad_in)

    grad_now = cotangent
    grad_input = zero_tok
    kept_grad = zero_tok
    kept_dgate = jnp.zeros((model_width, tok_rows), jnp.float32)
    kept_dpre = jnp.zeros((2 * model_width, tok_rows), jnp.bfloat16)
    for section_step in reversed(range(section_count)):
        active = section_index == section_step
        arriving = grad_now
        kept_grad = jnp.where(active, arriving, kept_grad)
        dmixed_tok, kept_dgate = lax.cond(
            active, lambda: grad_front(arriving), lambda previous=kept_dgate: (zero_cols, previous)
        )
        dmixed_chan = to_channels(dmixed_tok)
        dvalue_chan = lax.cond(active, lambda: channel_backward(dmixed_chan), lambda: zero_chan)
        dvalue_tok = to_tokens(dvalue_chan)
        dgate_now = kept_dgate
        kept_dpre, grad_input = lax.cond(
            active,
            lambda: grad_back(dvalue_tok, dgate_now, arriving),
            lambda previous=(kept_dpre, grad_input): previous,
        )
        if section_step > 0:
            grad_now = pass_section(grad_input, -1)
    inner_term = jnp.einsum("tr,et->re", normed, kept_dpre, preferred_element_type=jnp.float32)
    outer_term = jnp.einsum("et,tf->ef", kept_gated, kept_grad, preferred_element_type=jnp.float32)
    inner_sum, outer_sum = (
        lax.psum_scatter(inner_term, "seq", scatter_dimension=0, tiled=True),
        lax.psum_scatter(outer_term, "seq", scatter_dimension=0, tiled=True),
    )
    return (
        produced[None],
        grad_input[None],
        (inner_sum * grad_scale)[None],
        (outer_sum * grad_scale)[None],
    )


def solution(mesh):
    return jax.shard_map(
        on_device,
        mesh=mesh,
        in_specs=(
            P("seq", None),
            P("seq", None),
            P("section", None),
            P("section", None, None),
            P("section", None, None),
            P("section", None),
            P("section", None, None),
            P("section", None, None),
            P("section", None, "seq"),
            P("section", "seq"),
        ),
        out_specs=(
            P("section", "seq", None),
            P("section", "seq", None),
            P("section", "seq", None),
            P("section", "seq", None),
        ),
        check_vma=False,
    )
```

profile of v0, /device:TPU:1, one launch (start us, length us, event | category | flops | bytes accessed | tf_op | source)
XLA Modules:
  0.0 706.7 jit_solution(8830643134753684994)
XLA Ops:
  7.2 8.1 %conditional.24 = (f32[128,1]{0,1:T(1,128)S(1)}, bf16[128,1024]{1,0:T(8,128)(2,1)}, f32[2048,128]{0,1:T(8,128)}, bf16[1024,128]{0,1:T(8,128)(2,1)S(1)}) conditional(s32[]{:T(128)} %convert_element_type.963, () %tuple.187, (bf16[128,1024]{1,0:T(8,128)(2,1)}, f32[1,1024]{1,0:T(1,128)}, bf16[1024,2048]{1,0:T(8,128)(2,1)}) %tuple.481), branch_computations={%region_0.1_spmd, %region_1.3_spmd} | conditional | flops 538443904 | bytes 7084576 | solution.py:218
  16.1 6.4 all-to-all-start
  31.7 22.6 %conditional.25 = (bf16[128,1024]{0,1:T(8,128)(2,1)}) conditional(s32[]{:T(128)} %convert_element_type.963, () %tuple.189, (bf16[128,8,128]{2,0,1:T(8,128)(2,1)}, f32[128,32,64]{0,2,1:T(8,128)S(1)}, f32[128,1]{0,1:T(1,128)}) %tuple.190), branch_computations={%region_4.5_spmd, %region_5.7_spmd} | conditional | flops 1013114624 | bytes 32782576 | solution.py:222
  61.1 8.8 %all-to-all-done.1 = bf16[128,8,128]{2,0,1:T(8,128)(2,1)} async-done(((bf16[128,8,128]{2,0,1:T(8,128)(2,1)}), bf16[128,8,128]{2,0,1:T(8,128)(2,1)}, u32[]{:S(2)}, u32[]{:S(2)}) %all-to-all-start.1) | async-done | bytes 262176 | tf_op jit(solution)/shard_map/all_to_all | solution.py:162
  69.9 6.7 conditional.26
  84.4 5.5 all-to-all-start.2
  89.9 8.8 %all-to-all-done.2 = bf16[8,128,128]{2,1,0:T(8,128)(2,1)} async-done(((bf16[8,128,128]{2,1,0:T(8,128)(2,1)}), bf16[8,128,128]{2,1,0:T(8,128)(2,1)}, u32[]{:S(2)}, u32[]{:S(2)}) %all-to-all-start.2) | async-done | bytes 262176 | tf_op jit(solution)/shard_map/all_to_all | solution.py:159
  101.3 13.7 %all_to_all.286 = bf16[128,8,128]{2,0,1:T(8,128)(2,1)} all-to-all(bf16[128,8,128]{2,0,1:T(8,128)(2,1)} %copy.433), channel_id=1, replica_groups=mesh['section'=4,'seq'=8] {'seq'}, dimensions={1} | all-to-all | bytes 524288 | tf_op jit(solution)/shard_map/all_to_all | solution.py:162
  115.2 43.1 %collective-permute-start.1 = (bf16[128,1024]{1,0:T(8,128)(2,1)}, bf16[128,1024]{1,0:T(8,128)(2,1)}, u32[]{:S(2)}, u32[]{:S(2)}) collective-permute-start(bf16[128,1024]{1,0:T(8,128)(2,1)} %get-tuple-element.441), channel_id=1, source_target_pairs={{0,8},{8,16},{16,24},{1,9},{9,17},{17,25},{2,10},{10,18},{18,26},{... | collective-permute-start | bytes 786440 | tf_op jit(solution)/shard_map/ppermute | solution.py:15
  163.3 5.8 all-to-all-start.4
  169.1 8.8 %all-to-all-done.4 = bf16[8,128,128]{2,1,0:T(8,128)(2,1)} async-done(((bf16[8,128,128]{2,1,0:T(8,128)(2,1)}), bf16[8,128,128]{2,1,0:T(8,128)(2,1)}, u32[]{:S(2)}, u32[]{:S(2)}) %all-to-all-start.4) | async-done | bytes 262176 | tf_op jit(solution)/shard_map/all_to_all | solution.py:159
  180.4 13.7 %all_to_all.287 = bf16[128,8,128]{2,0,1:T(8,128)(2,1)} all-to-all(bf16[128,8,128]{2,0,1:T(8,128)(2,1)} %copy.437), channel_id=1, replica_groups=mesh['section'=4,'seq'=8] {'seq'}, dimensions={1} | all-to-all | bytes 524288 | tf_op jit(solution)/shard_map/all_to_all | solution.py:162
  209.6 8.7 %all-to-all-done.6 = bf16[8,128,128]{2,1,0:T(8,128)(2,1)S(1)} async-done(((bf16[8,128,128]{2,1,0:T(8,128)(2,1)}), bf16[8,128,128]{2,1,0:T(8,128)(2,1)S(1)}, u32[]{:S(2)}, u32[]{:S(2)}) %all-to-all-start.6) | async-done | bytes 262176 | tf_op jit(solution)/shard_map/all_to_all | solution.py:159
  223.6 8.7 %all-to-all-done.7 = bf16[128,8,128]{2,0,1:T(8,128)(2,1)S(1)} async-done(((bf16[128,8,128]{2,0,1:T(8,128)(2,1)}), bf16[128,8,128]{2,0,1:T(8,128)(2,1)S(1)}, u32[]{:S(2)}, u32[]{:S(2)}) %all-to-all-start.7) | async-done | bytes 262176 | tf_op jit(solution)/shard_map/all_to_all | solution.py:162
  240.4 8.7 %all-to-all-done.8 = bf16[8,128,128]{2,1,0:T(8,128)(2,1)S(1)} async-done(((bf16[8,128,128]{2,1,0:T(8,128)(2,1)}), bf16[8,128,128]{2,1,0:T(8,128)(2,1)S(1)}, u32[]{:S(2)}, u32[]{:S(2)}) %all-to-all-start.8) | async-done | bytes 262176 | tf_op jit(solution)/shard_map/all_to_all | solution.py:159
  256.0 7.8 %all-to-all-done.9 = bf16[128,8,128]{2,0,1:T(8,128)(2,1)} async-done(((bf16[128,8,128]{2,0,1:T(8,128)(2,1)}), bf16[128,8,128]{2,0,1:T(8,128)(2,1)}, u32[]{:S(2)}, u32[]{:S(2)}) %all-to-all-start.9) | async-done | bytes 262176 | tf_op jit(solution)/shard_map/all_to_all | solution.py:162
  267.0 45.6 %collective-permute-done.3 = bf16[128,1024]{1,0:T(8,128)(2,1)} collective-permute-done((bf16[128,1024]{1,0:T(8,128)(2,1)}, bf16[128,1024]{1,0:T(8,128)(2,1)}, u32[]{:S(2)}, u32[]{:S(2)}) %collective-permute-start.3) | collective-permute-done | bytes 262176 | tf_op jit(solution)/shard_map/ppermute | solution.py:15
  313.4 5.5 all-to-all-start.10
  318.9 8.8 %all-to-all-done.10 = bf16[8,128,128]{2,1,0:T(8,128)(2,1)} async-done(((bf16[8,128,128]{2,1,0:T(8,128)(2,1)}), bf16[8,128,128]{2,1,0:T(8,128)(2,1)}, u32[]{:S(2)}, u32[]{:S(2)}) %all-to-all-start.10) | async-done | bytes 262176 | tf_op jit(solution)/shard_map/all_to_all | solution.py:159
  330.3 13.7 %all_to_all.288 = bf16[128,8,128]{2,0,1:T(8,128)(2,1)} all-to-all(bf16[128,8,128]{2,0,1:T(8,128)(2,1)} %copy.449), channel_id=1, replica_groups=mesh['section'=4,'seq'=8] {'seq'}, dimensions={1} | all-to-all | bytes 524288 | tf_op jit(solution)/shard_map/all_to_all | solution.py:162
  345.5 9.7 %collective-permute-done.4 = bf16[128,1024]{1,0:T(8,128)(2,1)} collective-permute-done((bf16[128,1024]{1,0:T(8,128)(2,1)}, bf16[128,1024]{1,0:T(8,128)(2,1)}, u32[]{:S(2)}, u32[]{:S(2)}) %collective-permute-start.4) | collective-permute-done | bytes 262176 | tf_op jit(solution)/shard_map/ppermute | solution.py:15
  355.9 5.5 all-to-all-start.12
  361.4 8.8 %all-to-all-done.12 = bf16[8,128,128]{2,1,0:T(8,128)(2,1)} async-done(((bf16[8,128,128]{2,1,0:T(8,128)(2,1)}), bf16[8,128,128]{2,1,0:T(8,128)(2,1)}, u32[]{:S(2)}, u32[]{:S(2)}) %all-to-all-start.12) | async-done | bytes 262176 | tf_op jit(solution)/shard_map/all_to_all | solution.py:159
  372.8 13.7 %all_to_all.289 = bf16[128,8,128]{2,0,1:T(8,128)(2,1)} all-to-all(bf16[128,8,128]{2,0,1:T(8,128)(2,1)} %copy.453), channel_id=1, replica_groups=mesh['section'=4,'seq'=8] {'seq'}, dimensions={1} | all-to-all | bytes 524288 | tf_op jit(solution)/shard_map/all_to_all | solution.py:162
  388.0 145.0 %collective-permute-done.5 = bf16[128,1024]{1,0:T(8,128)(2,1)} collective-permute-done((bf16[128,1024]{1,0:T(8,128)(2,1)}, bf16[128,1024]{1,0:T(8,128)(2,1)}, u32[]{:S(2)}, u32[]{:S(2)}) %collective-permute-start.5) | collective-permute-done | bytes 262176 | tf_op jit(solution)/shard_map/ppermute | solution.py:15
  536.8 5.3 conditional.45
  547.1 13.6 %all-to-all-done.14 = bf16[8,128,128]{2,1,0:T(8,128)(2,1)S(1)} async-done(((bf16[8,128,128]{2,1,0:T(8,128)(2,1)}), bf16[8,128,128]{2,1,0:T(8,128)(2,1)S(1)}, u32[]{:S(2)}, u32[]{:S(2)}) %all-to-all-start.14) | async-done | bytes 262176 | tf_op jit(solution)/shard_map/all_to_all | solution.py:159
  560.6 19.1 %conditional.46 = (bf16[128,1024]{0,1:T(8,128)(2,1)}) conditional(s32[]{:T(128)} %convert_element_type.963, () %tuple.219, (bf16[128,8,128]{2,0,1:T(8,128)(2,1)S(1)}, f32[128,32,64]{0,2,1:T(8,128)S(1)}, f32[128,1]{0,1:T(1,128)S(1)}) %tuple.519), branch_computations={%region_59.60_spmd, %region_60.62_spmd} | conditional | flops 1013114624 | bytes 33855756 | solution.py:286
  583.8 12.4 %all-to-all-done.15 = bf16[128,8,128]{0,2,1:T(8,128)(2,1)S(1)} async-done(((bf16[128,8,128]{0,2,1:T(8,128)(2,1)}), bf16[128,8,128]{0,2,1:T(8,128)(2,1)S(1)}, u32[]{:S(2)}, u32[]{:S(2)}) %all-to-all-start.15) | async-done | bytes 262176 | tf_op jit(solution)/shard_map/all_to_all | solution.py:162
  596.2 10.1 %conditional.47 = (bf16[2048,128]{1,0:T(8,128)(2,1)}, bf16[1,128,1024]{2,1,0:T(8,128)(2,1)}) conditional(s32[]{:T(128)} %convert_element_type.963, (bf16[2048,128]{1,0:T(8,128)(2,1)}, bf16[128,1024]{1,0:T(8,128)(2,1)}) %get-tuple-element.1171, (f32[2048,128]{0,1:T(8,128)}, f32[1024,128]{1,0:T(8,128)}, bf16[8,128,128]{1,2,0:T(8,128)(2,1)S(1)}, ...), branch_computations={%region_62.63_spmd, %region_63.65_spmd} | conditional | flops 542113792 | bytes 12854316 | solution.py:289
  606.3 5.8 fusion.738
  614.1 83.0 %reduce-scatter.3.cloned.1.call-done = f32[128,2048]{1,0:T(8,128)} async-done(((f32[1024,2048]{1,0:T(8,128)}), f32[128,2048]{1,0:T(8,128)}) %reduce-scatter.3.cloned.1.call-update) | async-done | bytes 1048592 | tf_op jit(solution)/shard_map/reduce_scatter | solution.py:299
  (217 shorter events, 178.9 us)
Async XLA Ops:
  7.2 17.2 %copy-start = (f32[1,64,128]{2,1,0:T(8,128)S(1)}, f32[1,64,128]{2,1,0:T(8,128)}, u32[]{:S(2)}) copy-start(f32[1,64,128]{2,1,0:T(8,128)} %param.66) | copy-start | bytes 98308
  7.2 15.7 %copy-start.66 = (f32[1,128]{1,0:T(1,128)S(1)}, f32[1,128]{1,0:T(1,128)}, u32[]{:S(2)}) copy-start(f32[1,128]{1,0:T(1,128)} %param.67) | copy-start | bytes 1540
  7.2 15.7 %copy-start.65 = (s32[1,32]{1,0:T(1,128)S(1)}, s32[1,32]{1,0:T(1,128)}, u32[]{:S(2)}) copy-start(s32[1,32]{1,0:T(1,128)} %param.63) | copy-start | bytes 388
  7.2 16.3 %copy-start.58 = (f32[1,64,64]{2,1,0:T(8,128)S(1)}, f32[1,64,64]{2,1,0:T(8,128)}, u32[]{:S(2)}) copy-start(f32[1,64,64]{2,1,0:T(8,128)} %param.64) | copy-start | bytes 49156
  7.2 16.8 %copy-start.59 = (f32[1,64,64]{2,1,0:T(8,128)S(1)}, f32[1,64,64]{2,1,0:T(8,128)}, u32[]{:S(2)}) copy-start(f32[1,64,64]{2,1,0:T(8,128)} %param.65) | copy-start | bytes 49156
  15.3 12.9 %copy-start.60 = (f32[128,1]{0,1:T(1,128)}, f32[128,1]{0,1:T(1,128)S(1)}, u32[]{:S(2)}) copy-start(f32[128,1]{0,1:T(1,128)S(1)} %get-tuple-element.1199) | copy-start | bytes 1540
  16.1 15.5 %all-to-all-start = ((bf16[8,128,128]{2,1,0:T(8,128)(2,1)}), bf16[8,128,128]{2,1,0:T(8,128)(2,1)}, u32[]{:S(2)}, u32[]{:S(2)}) async-start(bf16[8,128,128]{2,1,0:T(8,128)(2,1)} %bitcast.122), calls=%async_computation | async-start | bytes 524288 | tf_op jit(solution)/shard_map/all_to_all | solution.py:159
  31.6 38.3 %copy-start.2 = (bf16[1,1024,1024]{2,1,0:T(8,128)(2,1)S(1)}, bf16[1,1024,1024]{2,1,0:T(8,128)(2,1)}, u32[]{:S(2)}) copy-start(bf16[1,1024,1024]{2,1,0:T(8,128)(2,1)} %param.62) | copy-start | bytes 6291460
  56.0 13.9 %all-to-all-start.1 = ((bf16[128,8,128]{2,0,1:T(8,128)(2,1)}), bf16[128,8,128]{2,0,1:T(8,128)(2,1)}, u32[]{:S(2)}, u32[]{:S(2)}) async-start(bf16[128,8,128]{2,0,1:T(8,128)(2,1)} %copy.429), calls=%async_computation.1 | async-start | bytes 524288 | tf_op jit(solution)/shard_map/all_to_all | solution.py:162
  69.9 13.2 %copy-start.8 = (f32[1,1024]{1,0:T(1,128)S(1)}, f32[1,1024]{1,0:T(1,128)}, u32[]{:S(2)}) copy-start(f32[1,1024]{1,0:T(1,128)} %param.60) | copy-start | bytes 12292
  76.6 6.5 collective-permute-start
  83.1 15.6 %copy-start.48 = (f32[128,1]{0,1:T(1,128)S(1)}, f32[128,1]{0,1:T(1,128)}, u32[]{:S(2)}) copy-start(f32[128,1]{0,1:T(1,128)} %convolution_bitcast_fusion.21) | copy-start | bytes 1540
  84.4 14.3 %all-to-all-start.2 = ((bf16[8,128,128]{2,1,0:T(8,128)(2,1)}), bf16[8,128,128]{2,1,0:T(8,128)(2,1)}, u32[]{:S(2)}, u32[]{:S(2)}) async-start(bf16[8,128,128]{2,1,0:T(8,128)(2,1)} %bitcast.456), calls=%async_computation.2 | async-start | bytes 524288 | tf_op jit(solution)/shard_map/all_to_all | solution.py:159
  115.2 47.3 %collective-permute-start.1 = (bf16[128,1024]{1,0:T(8,128)(2,1)}, bf16[128,1024]{1,0:T(8,128)(2,1)}, u32[]{:S(2)}, u32[]{:S(2)}) collective-permute-start(bf16[128,1024]{1,0:T(8,128)(2,1)} %get-tuple-element.441), channel_id=1, source_target_pairs={{0,8},{8,16},{16,24},{1,9},{9,17},{17,25},{2,10},{10,18},{18,26},{... | collective-permute-start | bytes 786440 | tf_op jit(solution)/shard_map/ppermute | solution.py:15
  163.3 14.6 %all-to-all-start.4 = ((bf16[8,128,128]{2,1,0:T(8,128)(2,1)}), bf16[8,128,128]{2,1,0:T(8,128)(2,1)}, u32[]{:S(2)}, u32[]{:S(2)}) async-start(bf16[8,128,128]{2,1,0:T(8,128)(2,1)} %bitcast.457), calls=%async_computation.4 | async-start | bytes 524288 | tf_op jit(solution)/shard_map/all_to_all | solution.py:159
  194.2 9.0 %collective-permute-start.2 = (bf16[128,1024]{1,0:T(8,128)(2,1)}, bf16[128,1024]{1,0:T(8,128)(2,1)}, u32[]{:S(2)}, u32[]{:S(2)}) collective-permute-start(bf16[128,1024]{1,0:T(8,128)(2,1)} %get-tuple-element.1155), channel_id=1, source_target_pairs={{0,8},{8,16},{16,24},{1,9},{9,17},{17,25},{2,10},{10,18},{18,26},{... | collective-permute-start | bytes 786440 | tf_op jit(solution)/shard_map/ppermute | solution.py:15
  204.4 13.9 %all-to-all-start.6 = ((bf16[8,128,128]{2,1,0:T(8,128)(2,1)}), bf16[8,128,128]{2,1,0:T(8,128)(2,1)S(1)}, u32[]{:S(2)}, u32[]{:S(2)}) async-start(bf16[8,128,128]{2,1,0:T(8,128)(2,1)} %bitcast.455), calls=%async_computation.6 | async-start | bytes 524288 | tf_op jit(solution)/shard_map/all_to_all | solution.py:159
  219.2 13.1 %all-to-all-start.7 = ((bf16[128,8,128]{2,0,1:T(8,128)(2,1)}), bf16[128,8,128]{2,0,1:T(8,128)(2,1)S(1)}, u32[]{:S(2)}, u32[]{:S(2)}) async-start(bf16[128,8,128]{2,0,1:T(8,128)(2,1)} %copy.441), calls=%async_computation.7 | async-start | bytes 524288 | tf_op jit(solution)/shard_map/all_to_all | solution.py:162
  236.0 13.1 %all-to-all-start.8 = ((bf16[8,128,128]{2,1,0:T(8,128)(2,1)}), bf16[8,128,128]{2,1,0:T(8,128)(2,1)S(1)}, u32[]{:S(2)}, u32[]{:S(2)}) async-start(bf16[8,128,128]{2,1,0:T(8,128)(2,1)} %bitcast.161), calls=%async_computation.8 | async-start | bytes 524288 | tf_op jit(solution)/shard_map/all_to_all | solution.py:159
  249.1 14.6 %copy-start.61 = (f32[128,1]{0,1:T(1,128)S(1)}, f32[128,1]{0,1:T(1,128)}, u32[]{:S(2)}) copy-start(f32[128,1]{0,1:T(1,128)} %get-tuple-element.450) | copy-start | bytes 1540
  250.0 13.8 %all-to-all-start.9 = ((bf16[128,8,128]{2,0,1:T(8,128)(2,1)}), bf16[128,8,128]{2,0,1:T(8,128)(2,1)}, u32[]{:S(2)}, u32[]{:S(2)}) async-start(bf16[128,8,128]{2,0,1:T(8,128)(2,1)} %copy.445), calls=%async_computation.9 | async-start | bytes 524288 | tf_op jit(solution)/shard_map/all_to_all | solution.py:162
  265.7 46.9 %collective-permute-start.3 = (bf16[128,1024]{1,0:T(8,128)(2,1)}, bf16[128,1024]{1,0:T(8,128)(2,1)}, u32[]{:S(2)}, u32[]{:S(2)}) collective-permute-start(bf16[128,1024]{1,0:T(8,128)(2,1)} %get-tuple-element.451), channel_id=1, source_target_pairs={{8,0},{16,8},{24,16},{9,1},{17,9},{25,17},{10,2},{18,10},{26,18},{... | collective-permute-start | bytes 786440 | tf_op jit(solution)/shard_map/ppermute | solution.py:15
  313.4 14.3 %all-to-all-start.10 = ((bf16[8,128,128]{2,1,0:T(8,128)(2,1)}), bf16[8,128,128]{2,1,0:T(8,128)(2,1)}, u32[]{:S(2)}, u32[]{:S(2)}) async-start(bf16[8,128,128]{2,1,0:T(8,128)(2,1)} %bitcast.166), calls=%async_computation.10 | async-start | bytes 524288 | tf_op jit(solution)/shard_map/all_to_all | solution.py:159
  344.2 11.0 %collective-permute-start.4 = (bf16[128,1024]{1,0:T(8,128)(2,1)}, bf16[128,1024]{1,0:T(8,128)(2,1)}, u32[]{:S(2)}, u32[]{:S(2)}) collective-permute-start(bf16[128,1024]{1,0:T(8,128)(2,1)} %get-tuple-element.454), channel_id=1, source_target_pairs={{8,0},{16,8},{24,16},{9,1},{17,9},{25,17},{10,2},{18,10},{26,18},{... | collective-permute-start | bytes 786440 | tf_op jit(solution)/shard_map/ppermute | solution.py:15
  355.9 14.3 %all-to-all-start.12 = ((bf16[8,128,128]{2,1,0:T(8,128)(2,1)}), bf16[8,128,128]{2,1,0:T(8,128)(2,1)}, u32[]{:S(2)}, u32[]{:S(2)}) async-start(bf16[8,128,128]{2,1,0:T(8,128)(2,1)} %bitcast.171), calls=%async_computation.12 | async-start | bytes 524288 | tf_op jit(solution)/shard_map/all_to_all | solution.py:159
  361.4 250.8 %reduce-scatter.5.cloned.1.call-start = ((), (), s32[]{:S(2)}) async-start(), calls=%async_computation.19 | async-start | bytes 4718592 | tf_op jit(solution)/shard_map/reduce_scatter | solution.py:300
  386.7 146.3 %collective-permute-start.5 = (bf16[128,1024]{1,0:T(8,128)(2,1)}, bf16[128,1024]{1,0:T(8,128)(2,1)}, u32[]{:S(2)}, u32[]{:S(2)}) collective-permute-start(bf16[128,1024]{1,0:T(8,128)(2,1)} %get-tuple-element.1157), channel_id=1, source_target_pairs={{8,0},{16,8},{24,16},{9,1},{17,9},{25,17},{10,2},{18,10},{26,18},{... | collective-permute-start | bytes 786440 | tf_op jit(solution)/shard_map/ppermute | solution.py:15
  542.1 18.5 %all-to-all-start.14 = ((bf16[8,128,128]{2,1,0:T(8,128)(2,1)}), bf16[8,128,128]{2,1,0:T(8,128)(2,1)S(1)}, u32[]{:S(2)}, u32[]{:S(2)}) async-start(bf16[8,128,128]{2,1,0:T(8,128)(2,1)} %bitcast.176), calls=%async_computation.14 | async-start | bytes 524288 | tf_op jit(solution)/shard_map/all_to_all | solution.py:159
  572.7 2.4 copy-start.15
  579.8 16.4 %all-to-all-start.15 = ((bf16[128,8,128]{0,2,1:T(8,128)(2,1)}), bf16[128,8,128]{0,2,1:T(8,128)(2,1)S(1)}, u32[]{:S(2)}, u32[]{:S(2)}) async-start(bf16[128,8,128]{0,2,1:T(8,128)(2,1)} %bitcast.178), calls=%async_computation.15 | async-start | bytes 524288 | tf_op jit(solution)/shard_map/all_to_all | solution.py:162
  583.8 113.3 %reduce-scatter.3.cloned.1.call-start = ((), (), s32[]{:S(2)}) async-start(), calls=%async_computation.18 | async-start | bytes 9437184 | tf_op jit(solution)/shard_map/reduce_scatter | solution.py:299
  612.2 87.2 %copy-start.1 = (f32[1,64,128]{2,1,0:T(8,128)S(1)}, f32[1,64,128]{2,1,0:T(8,128)}, u32[]{:S(2)}) copy-start(f32[1,64,128]{2,1,0:T(8,128)} %param.66) | copy-start | bytes 98308
  (14 other events, 12.9 us)
Sparse Core Ops, SparseCore 0:
  536.9 55.6 reduce-scatter.4
  612.3 84.7 reduce-scatter.2
where the time goes:
time: 719 us; the launch traced here: 707 us
  waiting for transfers between devices  400 us (56%)
  starting transfers between devices  115 us (16%)
  blocking collectives  54.9 us (8%)
  matrix products  48.4 us (7%)
  local copies, waits for them, and re-layouts  38.8 us (5%)
  other arithmetic  31.3 us (4%)
  between operations  14.8 us (2%)
    ppermute x6, waiting for transfers between devices, passed_along(): lax.ppermute(value, axis, [(source, source + steps) for source in range(i...  213 us
    reduce_scatter x1, waiting for transfers between devices, on_device(): lax.psum_scatter(inner_term, 'seq', scatter_dimension=0, tiled=True)  83 us
    all_to_all x8, waiting for transfers between devices, to_channels(): return lax.all_to_all(block, 'seq', split_axis=0, concat_axis=1, tiled=True)  66.2 us
    all_to_all x4, blocking collectives, to_tokens(): return lax.all_to_all(block, 'seq', split_axis=1, concat_axis=0, tiled=True)  54.9 us
    ppermute x6, starting transfers between devices, passed_along(): lax.ppermute(value, axis, [(source, source + steps) for source in range(i...  53.7 us
    all_to_all x8, starting transfers between devices, to_channels(): return lax.all_to_all(block, 'seq', split_axis=0, concat_axis=1, tiled=True)  43.3 us
    all_to_all x4, waiting for transfers between devices, to_tokens(): return lax.all_to_all(block, 'seq', split_axis=1, concat_axis=0, tiled=True)  37.6 us
    all_to_all x4, starting transfers between devices, to_tokens(): return lax.all_to_all(block, 'seq', split_axis=1, concat_axis=0, tiled=True)  18.5 us
  transfers between devices with their start and end apart: 20, of which 18 were waited for; matrix products, arithmetic and copies ran while one was open for 7% of the time, Pallas kernels for 0%

commit v1 on v0

--- a/solution.py
+++ b/solution.py
@@ -1,8 +1,12 @@
+import functools
 import math
 
 import jax
 import jax.numpy as jnp
+import numpy as np
 from jax import lax
+from jax.experimental import pallas as pl
+from jax.experimental.pallas import tpu as pltpu
 from jax.sharding import PartitionSpec as P
 
 EPSILON = 1e-06
@@ -138,7 +142,7 @@
     return (signal / fft_size).reshape(own_chans, half_rows * size_second)
 
 
-def on_device(
+def on_device_factored(
     tokens, cotangent, norm_gain, w_inner, w_outer, rpe_periods, rpe_in, rpe_mid, rpe_out, decay
 ):
     tok_rows, model_width = tokens.shape
@@ -305,6 +309,444 @@
         (inner_sum * grad_scale)[None],
         (outer_sum * grad_scale)[None],
     )
+
+
+def dense_tables(seq_length):
+    fft_size = 2 * seq_length
+    coarse = math.gcd(seq_length, 32)
+    fine = seq_length // coarse
+    place = np.arange(seq_length, dtype=np.int64)
+
+    def pair(freqs):
+        angles = 2.0 * np.pi / fft_size * (freqs[:, None] * place[None, :] % fft_size)
+        return (np.cos(angles).astype(np.float32), np.sin(angles).astype(np.float32))
+
+    high_cos, high_sin = pair(np.arange(coarse, dtype=np.int64) * fine)
+    low_cos, low_sin = pair(np.arange(fine, dtype=np.int64))
+    parity = (1.0 - 2.0 * (place % 2)).astype(np.float32)
+
+    def build(high, low, shape, freq_axis):
+        hc, hs = high
+        lc, ls = low
+        cos = (hc * lc - hs * ls).reshape(shape)
+        sin = -(hs * lc + hc * ls).reshape(shape)
+        freq = lax.broadcasted_iota(jnp.int32, shape, freq_axis)
+        signs = parity[None, :] if freq_axis == 0 else parity[:, None]
+        sin = jnp.where(freq == 0, signs, sin)
+        return jnp.concatenate([cos, sin], axis=freq_axis).astype(jnp.bfloat16)
+
+    analysis = build(
+        (jnp.asarray(high_cos)[:, None, :], jnp.asarray(high_sin)[:, None, :]),
+        (jnp.asarray(low_cos)[None], jnp.asarray(low_sin)[None]),
+        (seq_length, seq_length),
+        0,
+    )
+    return analysis
+
+
+def silu_pair(pre_act):
+    sigmoid_val = 1.0 / (1.0 + jnp.exp(-pre_act))
+    return pre_act * sigmoid_val, sigmoid_val * (1.0 + pre_act * (1.0 - sigmoid_val))
+
+
+def relay_kernel(
+    parts,
+    sections,
+    tok_ref,
+    cot_ref,
+    gain_ref,
+    wi_ref,
+    wo_ref,
+    ana_ref,
+    syn_ref,
+    spec_ref,
+    out_ref,
+    gin_ref,
+    res_ref,
+    xbuf,
+    gbuf,
+    gate_act,
+    gate_slope,
+    val_slope,
+    send_a,
+    chan_a,
+    zbuf,
+    mix_chan,
+    mix_tok,
+    send_b,
+    chan_b,
+    dval_chan,
+    dval_tok,
+    dgate_send,
+    dgate_chan,
+    arr_chan,
+    slope_chan,
+    normed_all,
+    gated_all,
+    res_send,
+    a2a_send,
+    a2a_recv,
+    own_sem,
+    gat_send,
+    gat_recv,
+    fwd_send,
+    fwd_recv,
+    hop_send,
+    hop_recv,
+):
+    f32, bf16 = jnp.float32, jnp.bfloat16
+    sec = lax.axis_index("section")
+    me = lax.axis_index("seq")
+    rows, width = tok_ref.shape
+    length = rows * parts
+    cols = width // parts
+
+    def ds(index, size):
+        return pl.ds(pl.multiple_of(index * size, size), size)
+
+    def peer(step):
+        return lax.rem(me + step, parts)
+
+    barrier = pltpu.get_barrier_semaphore()
+    for step in range(1, parts):
+        pl.semaphore_signal(barrier, inc=1, device_id={"seq": peer(step)})
+
+    for step in (1, sections - 1):
+        pl.semaphore_signal(
+            barrier, inc=1, device_id={"section": lax.rem(sec + step, sections)}
+        )
+    pl.semaphore_wait(barrier, parts + 1)
+
+    def exchange(slot, source, target):
+        copies = []
+        for step in range(1, parts):
+            copies.append(
+                pltpu.make_async_remote_copy(
+                    src_ref=source(peer(step)),
+                    dst_ref=target(me),
+                    send_sem=a2a_send.at[slot, step],
+                    recv_sem=a2a_recv.at[slot, step],
+                    device_id={"seq": peer(step)},
+                )
+            )
+        copies.append(pltpu.make_async_copy(source(me), target(me), own_sem.at[slot]))
+        return copies
+
+    def start(copies):
+        for copy in copies:
+            copy.start()
+
+    def arrive(copies):
+        for copy in copies[:-1]:
+            copy.wait_recv()
+        copies[-1].wait()
+
+    def left(copies):
+        for copy in copies[:-1]:
+            copy.wait_send()
+
+    def col_block(ref):
+        return lambda device: ref.at[:, ds(device, cols)]
+
+    def row_block(ref, size):
+        return lambda device: ref.at[ds(device, size), :]
+
+    def mix(source, target, sign):
+        half = spec_ref.shape[1]
+        chunk = min(half, 256)
+        signal = source[...]
+        for first in range(0, half, chunk):
+            band = slice(first, first + chunk)
+            real = jnp.dot(ana_ref[band, :], signal, preferred_element_type=f32)
+            imag = jnp.dot(
+                ana_ref[half + first : half + first + chunk, :], signal, preferred_element_type=f32
+            )
+            k_re, k_im, k_ny = spec_ref[0, band, :], spec_ref[1, band, :], spec_ref[2, band, :]
+            zbuf[band, :] = (real * k_re - sign * (imag * k_im)).astype(bf16)
+            zbuf[half + first : half + first + chunk, :] = (
+                sign * (real * k_im) + imag * k_ny
+            ).astype(bf16)
+        shaped = zbuf[...]
+        for first in range(0, length, chunk):
+            target[first : first + chunk, :] = jnp.dot(
+                syn_ref[first : first + chunk, :], shaped, preferred_element_type=f32
+            ).astype(bf16)
+
+    hop_fwd = pltpu.make_async_remote_copy(
+        src_ref=out_ref,
+        dst_ref=xbuf,
+        send_sem=hop_send.at[0],
+        recv_sem=hop_recv.at[0],
+        device_id={"section": jnp.minimum(sec + 1, sections - 1)},
+    )
+    hop_bwd = pltpu.make_async_remote_copy(
+        src_ref=gin_ref,
+        dst_ref=gbuf,
+        send_sem=hop_send.at[1],
+        recv_sem=hop_recv.at[1],
+        device_id={"section": jnp.maximum(sec - 1, 0)},
+    )
+
+    @pl.when(sec == 0)
+    def _():
+        xbuf[...] = tok_ref[...]
+
+    @pl.when(sec > 0)
+    def _():
+        hop_fwd.wait_recv()
+
+    gain = gain_ref[...]
+    own_rows = ds(me, rows)
+
+    x_float = xbuf[...].astype(f32)
+    inv_rms = lax.rsqrt(jnp.mean(x_float * x_float, axis=1, keepdims=True) + EPSILON)
+    normed = (x_float * inv_rms * gain).astype(bf16)
+    normed_all[own_rows, :] = normed
+    pre_val = jnp.dot(normed, wi_ref[:, width:], preferred_element_type=f32)
+    act, slope = silu_pair(pre_val)
+    send_a[...] = act.astype(bf16)
+    to_chan = exchange(0, col_block(send_a), row_block(chan_a, rows))
+    start(to_chan)
+    val_slope[...] = slope.astype(bf16)
+    pre_gate = jnp.dot(normed, wi_ref[:, :width], preferred_element_type=f32)
+    act, slope = silu_pair(pre_gate)
+    gate_act[...] = act.astype(bf16)
+    gate_slope[...] = slope
+    arrive(to_chan)
+    mix(chan_a, mix_chan, 1.0)
+    to_tok = exchange(1, row_block(mix_chan, rows), col_block(mix_tok))
+    start(to_tok)
+    arrive(to_tok)
+    gated = (gate_act[...].astype(f32) * mix_tok[...].astype(f32)).astype(bf16)
+    gated_all[own_rows, :] = gated
+    update = jnp.dot(gated, wo_ref[...], preferred_element_type=f32)
+    out_ref[...] = (xbuf[...].astype(f32) + update).astype(bf16)
+
+    @pl.when(sec < sections - 1)
+    def _():
+        hop_fwd.start()
+
+    left(to_chan)
+    left(to_tok)
+
+    slope_move = exchange(2, col_block(val_slope), row_block(slope_chan, rows))
+    partner = me + 1 - 2 * lax.rem(me, 2)
+    chips = parts // 2
+    far, near = [], []
+    for index, ref in enumerate((normed_all, gated_all)):
+        for step in range(chips):
+            owner = lax.rem(me + parts - 2 * step, parts)
+            if step > 0:
+                far.append(
+                    pltpu.make_async_remote_copy(
+                        src_ref=ref.at[own_rows, :],
+                        dst_ref=ref.at[own_rows, :],
+                        send_sem=gat_send.at[index, step],
+                        recv_sem=gat_recv.at[index, step],
+                        device_id={"seq": peer(2 * step)},
+                    )
+                )
+            near.append(
+                pltpu.make_async_remote_copy(
+                    src_ref=ref.at[ds(owner, rows), :],
+                    dst_ref=ref.at[ds(owner, rows), :],
+                    send_sem=fwd_send.at[index, step],
+                    recv_sem=fwd_recv.at[index, step],
+                    device_id={"seq": partner},
+                )
+            )
+
+    def gather():
+        start(slope_move)
+        start(far)
+        for index in range(2):
+            near[index * chips].start()
+            for step in range(1, chips):
+                far[index * (chips - 1) + step - 1].wait_recv()
+                near[index * chips + step].start()
+        for copy in near:
+            copy.wait()
+        for copy in far:
+            copy.wait_send()
+        arrive(slope_move)
+        left(slope_move)
+
+    early = sections // 2
+
+    @pl.when(sec < early)
+    def _():
+        gather()
+
+    @pl.when(sec == sections - 1)
+    def _():
+        gbuf[...] = cot_ref[...]
+
+    @pl.when(sec < sections - 1)
+    def _():
+        hop_bwd.wait_recv()
+
+    contract_last = (((1,), (1,)), ((), ()))
+    contract_first = (((0,), (0,)), ((), ()))
+    dgated = lax.dot_general(gbuf[...], wo_ref[...], contract_last, preferred_element_type=f32)
+    send_b[...] = (dgated * gate_act[...].astype(f32)).astype(bf16)
+    grad_chan = exchange(3, col_block(send_b), row_block(chan_b, rows))
+    start(grad_chan)
+    dpre_gate = (dgated * mix_tok[...].astype(f32) * gate_slope[...]).astype(bf16)
+    dgate_send[...] = dpre_gate
+    dnormed_gate = lax.dot_general(
+        dpre_gate, wi_ref[:, :width], contract_last, preferred_element_type=f32
+    )
+    arrive(grad_chan)
+    arr_move = exchange(4, col_block(gbuf), row_block(arr_chan, rows))
+    dgate_move = exchange(5, col_block(dgate_send), row_block(dgate_chan, rows))
+    mix(chan_b, dval_chan, -1.0)
+    grad_tok = exchange(6, row_block(dval_chan, rows), col_block(dval_tok))
+    start(grad_tok)
+    start(arr_move)
+    start(dgate_move)
+
+    def result(part, lhs, rhs):
+        piece = lax.dot_general(lhs, rhs[...], contract_first, preferred_element_type=f32)
+        res_send[part] = piece.astype(bf16)
+
+    arrive(grad_tok)
+    dpre_val = (dval_tok[...].astype(f32) * val_slope[...].astype(f32)).astype(bf16)
+    dnormed = dnormed_gate + lax.dot_general(
+        dpre_val, wi_ref[:, width:], contract_last, preferred_element_type=f32
+    )
+    x_float = xbuf[...].astype(f32)
+    inv_rms = lax.rsqrt(jnp.mean(x_float * x_float, axis=1, keepdims=True) + EPSILON)
+    dscaled = dnormed * gain
+    x_hat = x_float * inv_rms
+    shared = jnp.mean(dscaled * x_hat, axis=1, keepdims=True)
+    gin_ref[...] = (gbuf[...].astype(f32) + inv_rms * (dscaled - x_hat * shared)).astype(bf16)
+
+    @pl.when(sec > 0)
+    def _():
+        hop_bwd.start()
+
+    @pl.when(sec >= early)
+    def _():
+        gather()
+
+    moves = []
+    for part in range(3):
+        if part == 0:
+            dval = (dval_chan[...].astype(f32) * slope_chan[...].astype(f32)).astype(bf16)
+            result(0, dval, normed_all)
+        elif part == 1:
+            arrive(arr_move)
+            result(1, arr_chan[...], gated_all)
+        else:
+            arrive(dgate_move)
+            result(2, dgate_chan[...], normed_all)
+        move = exchange(
+            7 + part,
+            lambda device, part=part: res_send.at[part, :, ds(device, cols)],
+            lambda device, part=part: res_ref.at[part, ds(device, cols), :],
+        )
+        start(move)
+        moves.append(move)
+    for move in moves:
+        arrive(move)
+        left(move)
+    for move in (grad_chan, grad_tok, arr_move, dgate_move):
+        left(move)
+
+    @pl.when(sec < sections - 1)
+    def _():
+        hop_fwd.wait_send()
+
+    @pl.when(sec > 0)
+    def _():
+        hop_bwd.wait_send()
+
+
+def on_device(
+    tokens, cotangent, norm_gain, w_inner, w_outer, rpe_periods, rpe_in, rpe_mid, rpe_out, decay
+):
+    rows, width = tokens.shape
+    parts = lax.axis_size("seq")
+    sections = lax.axis_size("section")
+    cols = width // parts
+    length = rows * parts
+    if cols % 128 or rows % 128 or length > 1024 or parts % 2 or sections < 2:
+        return on_device_factored(
+            tokens, cotangent, norm_gain, w_inner, w_outer, rpe_periods, rpe_in, rpe_mid, rpe_out, decay
+        )
+    bf16, f32 = jnp.bfloat16, jnp.float32
+    analysis = lax.optimization_barrier(dense_tables(length))
+    synthesis = analysis.T
+    kernel = kernel_rows(rpe_periods[0], rpe_in[0], rpe_mid[0], rpe_out[0], decay[0], length)
+    spec = lax.dot_general(
+        analysis, kernel.astype(bf16), (((1,), (1,)), ((), ())), preferred_element_type=f32
+    )
+    first = lax.broadcasted_iota(jnp.int32, (length, 1), 0) == 0
+    scale = jnp.where(first, 0.5, 1.0) / length
+    real, imag = spec[:length] * scale, spec[length:] * scale
+    spec = jnp.stack([real, jnp.where(first, 0.0, imag), jnp.where(first, imag, real)])
+    tok_block = lambda kind: pltpu.VMEM((rows, width), kind)
+    chan_block = lambda kind: pltpu.VMEM((length, cols), kind)
+    vmem = pl.BlockSpec(memory_space=pltpu.VMEM)
+    dma = pltpu.SemaphoreType.DMA
+    out, grad_in, res = pl.pallas_call(
+        functools.partial(relay_kernel, parts, sections),
+        out_shape=(
+            jax.ShapeDtypeStruct((rows, width), bf16),
+            jax.ShapeDtypeStruct((rows, width), bf16),
+            jax.ShapeDtypeStruct((3, width, cols), bf16),
+        ),
+        in_specs=[vmem] * 8,
+        out_specs=(vmem,) * 3,
+        scratch_shapes=[
+            tok_block(bf16),
+            tok_block(bf16),
+            tok_block(bf16),
+            tok_block(f32),
+            tok_block(bf16),
+            tok_block(bf16),
+            chan_block(bf16),
+            pltpu.VMEM((2 * length, cols), bf16),
+            chan_block(bf16),
+            tok_block(bf16),
+            tok_block(bf16),
+            chan_block(bf16),
+            chan_block(bf16),
+            tok_block(bf16),
+            tok_block(bf16),
+            chan_block(bf16),
+            chan_block(bf16),
+            chan_block(bf16),
+            pltpu.VMEM((length, width), bf16),
+            pltpu.VMEM((length, width), bf16),
+            pltpu.VMEM((3, cols, width), bf16),
+            dma((10, parts)),
+            dma((10, parts)),
+            dma((10,)),
+            dma((2, parts // 2)),
+            dma((2, parts // 2)),
+            dma((2, parts // 2)),
+            dma((2, parts // 2)),
+            dma((2,)),
+            dma((2,)),
+        ],
+        compiler_params=pltpu.CompilerParams(
+            collective_id=0, has_side_effects=True, vmem_limit_bytes=60 * 1024 * 1024
+        ),
+    )(
+        tokens,
+        cotangent,
+        norm_gain,
+        w_inner[0],
+        w_outer[0],
+        analysis,
+        synthesis,
+        spec,
+    )
+    grad_scale = 1.0 / math.sqrt(length)
+    inner = jnp.concatenate([res[2], res[0]], axis=0).T.astype(f32) * grad_scale
+    outer = res[1].T.astype(f32) * grad_scale
+    return (out[None], grad_in[None], inner[None], outer[None])
 
 
 def solution(mesh):

time: 719 us -> 267 us (0.37); the launches traced: 707 us -> 265 us
  waiting for transfers between devices: 400 us -> 0 us
  Pallas kernels: 0 us -> 230 us
  starting transfers between devices: 115 us -> 0 us
  blocking collectives: 54.9 us -> 0 us
  matrix products: 48.4 us -> 4.93 us
  local copies, waits for them, and re-layouts: 38.8 us -> 16.7 us
  other arithmetic: 31.3 us -> 13.2 us
  between operations: 14.8 us -> 0.82 us
    pallas_call x0 -> x1, Pallas kernels: none -> 230 us  [on_device(): pl.pallas_call(functools.partial(relay_kernel, parts, sections), out_shap...]
    ppermute x6 -> x0, waiting for transfers between devices: 213 us -> none  [passed_along(): lax.ppermute(value, axis, [(source, source + steps) for source in range(i...]
    all_to_all x12 -> x0, waiting for transfers between devices: 104 us -> none  [the longest x8 66.2 us: to_channels(): return lax.all_to_all(block, 'seq', split_axis=0, concat_axis=1, tiled=True)]
    reduce_scatter x2 -> x0, waiting for transfers between devices: 83 us -> none  [the longest x1 83 us: on_device(): lax.psum_scatter(inner_term, 'seq', scatter_dimension=0, tiled=True)]
    all_to_all x12 -> x0, starting transfers between devices: 61.7 us -> none  [the longest x8 43.3 us: to_channels(): return lax.all_to_all(block, 'seq', split_axis=0, concat_axis=1, tiled=True)]
    all_to_all x4 -> x0, blocking collectives: 54.9 us -> none  [to_tokens(): return lax.all_to_all(block, 'seq', split_axis=1, concat_axis=0, tiled=True)]
    ppermute x6 -> x0, starting transfers between devices: 53.7 us -> none  [passed_along(): lax.ppermute(value, axis, [(source, source + steps) for source in range(i...]
    dot_general x19 -> x1, matrix products: 46.5 us -> 1.29 us  [on_device(): lax.dot_general(analysis, kernel.astype(bf16), (((1,), (1,)), ((), ())),...]
  transfers between devices with their start and end apart: 20 -> 0, of which waited for: 18 -> 0; matrix products, arithmetic and copies ran while one was open for 7% -> 0% of each run, Pallas kernels for 0% -> 0%
where the time goes in v1:
time: 267 us; the launch traced here: 265 us
  Pallas kernels  230 us (86%)
  local copies, waits for them, and re-layouts  16.7 us (6%)
  other arithmetic  13.2 us (5%)
  matrix products  4.93 us (2%)
    pallas_call x1, Pallas kernels, on_device(): pl.pallas_call(functools.partial(relay_kernel, parts, sections), out_shap...  230 us
    optimization_barrier x1, local copies, waits for them, and re-layouts, on_device(): analysis = lax.optimization_barrier(dense_tables(length))  6.41 us

profile of v1, /device:TPU:1, one launch (start us, length us, event | category | flops | bytes accessed | tf_op | source)
XLA Modules:
  0.0 265.2 jit_solution(10821675569429398310)
XLA Ops:
  0.6 0.0 copy-start
  0.7 0.7 sqrt_bitcast_fusion
  1.3 1.3 fusion.14
  2.6 1.8 convolution_maximum_fusion
  4.4 0.0 copy-start.8
  4.4 1.3 convolution_maximum_fusion.1
  5.7 0.0 copy-done
  5.7 0.6 fusion.2
  6.3 1.9 add_negate_fusion
  8.1 0.0 copy-start.2
  8.2 0.0 copy-start.3
  8.2 0.0 copy-start.4
  8.2 0.0 copy-start.5
  8.2 2.6 copy.22
  10.8 3.1 %select_convert_fusion = bf16[1024,1024]{0,1:T(8,128)(2,1)} fusion(bf16[1024,1024]{0,1:T(8,128)(2,1)} %copy.22, bf16[1024]{0:T(1024)(128)(2,1)S(1)} %copy-done.8, pred[1024]{0:T(1024)(128)(4,1)S(1)} %iota_compare_fusion), kind=kLoop, calls=%fused_computation.1 | loop fusion | flops 1048576 | bytes 4197376 | tf_op jit(solution)/shard_map/convert.1
  13.9 0.8 subtract_convert_fusion
  14.7 2.6 copy.23
  17.3 2.7 %pad_maximum_fusion = bf16[2048,1024]{0,1:T(8,128)(2,1)S(1)} fusion(bf16[1024,1024]{0,1:T(8,128)(2,1)} %select_convert_fusion, bf16[1024,1024]{0,1:T(8,128)(2,1)} %copy.23), kind=kLoop, calls=%fused_computation | loop fusion | flops 8388608 | bytes 8388608 | tf_op jit(solution)/shard_map/concatenate | solution.py:336
  20.0 1.3 fusion.19
  21.3 0.3 select_bitcast_fusion.1
  21.7 0.3 copy-done.1
  22.0 1.3 pad_maximum_fusion.1.spec_ref
  23.3 6.4 %copy.24.ana_ref = bf16[2048,1024]{1,0:T(8,128)(2,1)} copy(bf16[2048,1024]{0,1:T(8,128)(2,1)} %copy-done.1) | data formatting | bytes 8388608 | tf_op jit(solution)/shard_map/optimization_barrier | solution.py:678
  29.7 229.6 %shard_map.174 = (bf16[128,1024]{1,0:T(8,128)(2,1)}, bf16[128,1024]{1,0:T(8,128)(2,1)}, bf16[3,1024,128]{2,1,0:T(8,128)(2,1)}) custom-call(bf16[128,1024]{1,0:T(8,128)(2,1)} %tok_ref.1, bf16[128,1024]{1,0:T(8,128)(2,1)} %cot_ref.1, f32[1,1024]{1,0:T(1,128)} %gain_ref.1, bf16[1024,2048]{1,0:T(8,128)(2,1)} %bitcast.54, bf16[1024,1024]{1,0:T(8,128)(2,1)} %bitcast.55, ...), custom_call_target="tpu_custom_call" | custom-call | tf_op jit(solution)/shard_map/pallas_call | solution.py:692
  259.3 1.0 multiply_bitcast_fusion.1
  260.3 1.1 slice_bitcast_fusion.1
  261.4 1.0 copy.26
  262.4 0.1 multiply_bitcast_fusion
  262.5 1.3 copy.25
  263.8 0.7 copy.29
  264.5 0.0 copy-done.6
  264.5 0.7 copy.30
  (12 shorter events, 0.0 us)
Async XLA Ops:
  0.6 5.1 %copy-start = (f32[1,64,128]{2,1,0:T(8,128)S(1)}, f32[1,64,128]{2,1,0:T(8,128)}, u32[]{:S(2)}) copy-start(f32[1,64,128]{2,1,0:T(8,128)} %param.23) | copy-start | bytes 98308
  4.4 6.4 %copy-start.8 = (bf16[1024]{0:T(1024)(128)(2,1)S(1)}, bf16[1024]{0:T(1024)(128)(2,1)}, u32[]{:S(2)}) copy-start(bf16[1024]{0:T(1024)(128)(2,1)} %constant.95) | copy-start | bytes 6148
  8.1 5.7 %copy-start.2 = (f32[32,1024]{1,0:T(8,128)S(1)}, f32[32,1024]{1,0:T(8,128)}, u32[]{:S(2)}) copy-start(f32[32,1024]{1,0:T(8,128)} %constant.50.clone) | copy-start | bytes 393220
  8.2 5.7 %copy-start.3 = (f32[32,1024]{1,0:T(8,128)S(1)}, f32[32,1024]{1,0:T(8,128)}, u32[]{:S(2)}) copy-start(f32[32,1024]{1,0:T(8,128)} %constant.49.clone) | copy-start | bytes 393220
  8.2 5.7 %copy-start.4 = (f32[32,1024]{1,0:T(8,128)S(1)}, f32[32,1024]{1,0:T(8,128)}, u32[]{:S(2)}) copy-start(f32[32,1024]{1,0:T(8,128)} %constant.48.clone) | copy-start | bytes 393220
  8.2 5.7 %copy-start.5 = (f32[32,1024]{1,0:T(8,128)S(1)}, f32[32,1024]{1,0:T(8,128)}, u32[]{:S(2)}) copy-start(f32[32,1024]{1,0:T(8,128)} %constant.47.clone) | copy-start | bytes 393220
  20.0 2.0 copy-start.1
  259.3 4.5 %copy-start.7 = (bf16[128,1024]{1,0:T(8,128)(2,1)S(1)}, bf16[128,1024]{1,0:T(8,128)(2,1)}, u32[]{:S(2)}) copy-start(bf16[128,1024]{1,0:T(8,128)(2,1)} %get-tuple-element.7) | copy-start | bytes 786436
  259.3 5.2 %copy-start.6 = (bf16[128,1024]{1,0:T(8,128)(2,1)S(1)}, bf16[128,1024]{1,0:T(8,128)(2,1)}, u32[]{:S(2)}) copy-start(bf16[128,1024]{1,0:T(8,128)(2,1)} %get-tuple-element.8) | copy-start | bytes 786436

commit v2 on v1

--- a/solution.py
+++ b/solution.py
@@ -311,6 +311,9 @@
     )
 
 
+SPLITS = 2
+
+
 def dense_tables(seq_length):
     fft_size = 2 * seq_length
     coarse = math.gcd(seq_length, 32)
@@ -323,25 +326,13 @@
 
     high_cos, high_sin = pair(np.arange(coarse, dtype=np.int64) * fine)
     low_cos, low_sin = pair(np.arange(fine, dtype=np.int64))
-    parity = (1.0 - 2.0 * (place % 2)).astype(np.float32)
-
-    def build(high, low, shape, freq_axis):
-        hc, hs = high
-        lc, ls = low
-        cos = (hc * lc - hs * ls).reshape(shape)
-        sin = -(hs * lc + hc * ls).reshape(shape)
-        freq = lax.broadcasted_iota(jnp.int32, shape, freq_axis)
-        signs = parity[None, :] if freq_axis == 0 else parity[:, None]
-        sin = jnp.where(freq == 0, signs, sin)
-        return jnp.concatenate([cos, sin], axis=freq_axis).astype(jnp.bfloat16)
-
-    analysis = build(
-        (jnp.asarray(high_cos)[:, None, :], jnp.asarray(high_sin)[:, None, :]),
-        (jnp.asarray(low_cos)[None], jnp.asarray(low_sin)[None]),
-        (seq_length, seq_length),
-        0,
-    )
-    return analysis
+    parity = np.broadcast_to((1.0 - 2.0 * (place % 2)).astype(np.float32), (16, seq_length))
+    shape = (seq_length, seq_length)
+    hc, hs = jnp.asarray(high_cos)[:, None, :], jnp.asarray(high_sin)[:, None, :]
+    lc, ls = jnp.asarray(low_cos)[None], jnp.asarray(low_sin)[None]
+    cos = (hc * lc - hs * ls).reshape(shape).astype(jnp.bfloat16)
+    sin = (-(hs * lc + hc * ls)).reshape(shape).astype(jnp.bfloat16)
+    return cos, sin, jnp.asarray(parity).astype(jnp.bfloat16)
 
 
 def silu_pair(pre_act):
@@ -357,8 +348,9 @@
     gain_ref,
     wi_ref,
     wo_ref,
-    ana_ref,
-    syn_ref,
+    cos_ref,
+    sin_ref,
+    par_ref,
     spec_ref,
     out_ref,
     gin_ref,
@@ -384,6 +376,9 @@
     normed_all,
     gated_all,
     res_send,
+    wo_t,
+    wi_t,
+    dnormed_gate,
     a2a_send,
     a2a_recv,
     own_sem,
@@ -400,6 +395,8 @@
     rows, width = tok_ref.shape
     length = rows * parts
     cols = width // parts
+    splits = hop_send.shape[1]
+    bands = [slice(i * rows // splits, (i + 1) * rows // splits) for i in range(splits)]
 
     def ds(index, size):
         return pl.ds(pl.multiple_of(index * size, size), size)
@@ -455,37 +452,48 @@
         half = spec_ref.shape[1]
         chunk = min(half, 256)
         signal = source[...]
+        nyquist = jnp.dot(par_ref[...], signal, preferred_element_type=f32)[:1, :]
         for first in range(0, half, chunk):
             band = slice(first, first + chunk)
-            real = jnp.dot(ana_ref[band, :], signal, preferred_element_type=f32)
-            imag = jnp.dot(
-                ana_ref[half + first : half + first + chunk, :], signal, preferred_element_type=f32
-            )
+            real = jnp.dot(cos_ref[band, :], signal, preferred_element_type=f32)
+            imag = jnp.dot(sin_ref[band, :], signal, preferred_element_type=f32)
+            if first == 0:
+                lead = lax.broadcasted_iota(jnp.int32, imag.shape, 0) == 0
+                imag = jnp.where(lead, nyquist, imag)
             k_re, k_im, k_ny = spec_ref[0, band, :], spec_ref[1, band, :], spec_ref[2, band, :]
             zbuf[band, :] = (real * k_re - sign * (imag * k_im)).astype(bf16)
             zbuf[half + first : half + first + chunk, :] = (
                 sign * (real * k_im) + imag * k_ny
             ).astype(bf16)
-        shaped = zbuf[...]
+        z_re, z_im = zbuf[:half, :], zbuf[half:, :]
+        z_ny = zbuf[half : half + 1, :].astype(f32)
         for first in range(0, length, chunk):
-            target[first : first + chunk, :] = jnp.dot(
-                syn_ref[first : first + chunk, :], shaped, preferred_element_type=f32
-            ).astype(bf16)
-
-    hop_fwd = pltpu.make_async_remote_copy(
-        src_ref=out_ref,
-        dst_ref=xbuf,
-        send_sem=hop_send.at[0],
-        recv_sem=hop_recv.at[0],
-        device_id={"section": jnp.minimum(sec + 1, sections - 1)},
-    )
-    hop_bwd = pltpu.make_async_remote_copy(
-        src_ref=gin_ref,
-        dst_ref=gbuf,
-        send_sem=hop_send.at[1],
-        recv_sem=hop_recv.at[1],
-        device_id={"section": jnp.maximum(sec - 1, 0)},
-    )
+            band = slice(first, first + chunk)
+            total = jnp.dot(cos_ref[band, :], z_re, preferred_element_type=f32)
+            total += jnp.dot(sin_ref[band, :], z_im, preferred_element_type=f32)
+            odd = lax.broadcasted_iota(jnp.int32, total.shape, 0) % 2 == 1
+            target[band, :] = (total + jnp.where(odd, -z_ny, z_ny)).astype(bf16)
+
+    def hop(direction, ref, landing, to_section):
+        return [
+            pltpu.make_async_remote_copy(
+                src_ref=ref.at[band, :],
+                dst_ref=landing.at[band, :],
+                send_sem=hop_send.at[direction, index],
+                recv_sem=hop_recv.at[direction, index],
+                device_id={"section": to_section},
+            )
+            for index, band in enumerate(bands)
+        ]
+
+    hop_fwd = hop(0, out_ref, xbuf, jnp.minimum(sec + 1, sections - 1))
+    hop_bwd = hop(1, gin_ref, gbuf, jnp.maximum(sec - 1, 0))
+
+    def transpose_weights():
+        for first in range(0, width, 256):
+            band = slice(first, first + 256)
+            wo_t[:, band] = wo_ref[band, :].T
+            wi_t[:, band] = wi_ref[band, :].T
 
     @pl.when(sec == 0)
     def _():
@@ -493,43 +501,81 @@
 
     @pl.when(sec > 0)
     def _():
-        hop_fwd.wait_recv()
+        transpose_weights()
 
     gain = gain_ref[...]
+
+    def scaled(band):
+        x_float = xbuf[band, :].astype(f32)
+        inv_rms = lax.rsqrt(jnp.mean(x_float * x_float, axis=1, keepdims=True) + EPSILON)
+        return x_float * inv_rms, inv_rms
+
+    def own(band):
+        size = band.stop - band.start
+        return pl.ds(pl.multiple_of(me * rows + band.start, size), size)
+
+    def cols_at(ref, band):
+        return lambda device: ref.at[band, ds(device, cols)]
+
+    def rows_at(ref, band):
+        size = band.stop - band.start
+        return lambda device: ref.at[
+            pl.ds(pl.multiple_of(device * rows + band.start, size), size), :
+        ]
+
+    to_chan, to_tok, grad_chan, grad_tok = [], [], [], []
+    for index, band in enumerate(bands):
+        to_chan.append(exchange(index, cols_at(send_a, band), rows_at(chan_a, band)))
+        to_tok.append(exchange(splits + index, rows_at(mix_chan, band), cols_at(mix_tok, band)))
+        grad_chan.append(
+            exchange(2 * splits + index, cols_at(send_b, band), rows_at(chan_b, band))
+        )
+        grad_tok.append(
+            exchange(3 * splits + index, rows_at(dval_chan, band), cols_at(dval_tok, band))
+        )
+    extra = 4 * splits
+    slope_move = exchange(extra, col_block(val_slope), row_block(slope_chan, rows))
+    arr_move = exchange(extra + 1, col_block(gbuf), row_block(arr_chan, rows))
+    dgate_move = exchange(extra + 2, col_block(dgate_send), row_block(dgate_chan, rows))
+
+    for index, band in enumerate(bands):
+
+        @pl.when(sec > 0)
+        def _():
+            hop_fwd[index].wait_recv()
+
+        x_hat, _ = scaled(band)
+        normed = (x_hat * gain).astype(bf16)
+        normed_all[own(band), :] = normed
+        pre_val = jnp.dot(normed, wi_ref[:, width:], preferred_element_type=f32)
+        act, slope = silu_pair(pre_val)
+        send_a[band, :] = act.astype(bf16)
+        start(to_chan[index])
+        val_slope[band, :] = slope.astype(bf16)
     own_rows = ds(me, rows)
-
-    x_float = xbuf[...].astype(f32)
-    inv_rms = lax.rsqrt(jnp.mean(x_float * x_float, axis=1, keepdims=True) + EPSILON)
-    normed = (x_float * inv_rms * gain).astype(bf16)
-    normed_all[own_rows, :] = normed
-    pre_val = jnp.dot(normed, wi_ref[:, width:], preferred_element_type=f32)
-    act, slope = silu_pair(pre_val)
-    send_a[...] = act.astype(bf16)
-    to_chan = exchange(0, col_block(send_a), row_block(chan_a, rows))
-    start(to_chan)
-    val_slope[...] = slope.astype(bf16)
-    pre_gate = jnp.dot(normed, wi_ref[:, :width], preferred_element_type=f32)
+    pre_gate = jnp.dot(normed_all[own_rows, :], wi_ref[:, :width], preferred_element_type=f32)
     act, slope = silu_pair(pre_gate)
     gate_act[...] = act.astype(bf16)
     gate_slope[...] = slope
-    arrive(to_chan)
+    for move in to_chan:
+        arrive(move)
     mix(chan_a, mix_chan, 1.0)
-    to_tok = exchange(1, row_block(mix_chan, rows), col_block(mix_tok))
-    start(to_tok)
-    arrive(to_tok)
-    gated = (gate_act[...].astype(f32) * mix_tok[...].astype(f32)).astype(bf16)
-    gated_all[own_rows, :] = gated
-    update = jnp.dot(gated, wo_ref[...], preferred_element_type=f32)
-    out_ref[...] = (xbuf[...].astype(f32) + update).astype(bf16)
-
-    @pl.when(sec < sections - 1)
-    def _():
-        hop_fwd.start()
-
-    left(to_chan)
-    left(to_tok)
-
-    slope_move = exchange(2, col_block(val_slope), row_block(slope_chan, rows))
+    for move in to_tok:
+        start(move)
+    for index, band in enumerate(bands):
+        arrive(to_tok[index])
+        gated = (gate_act[band, :].astype(f32) * mix_tok[band, :].astype(f32)).astype(bf16)
+        gated_all[own(band), :] = gated
+        update = jnp.dot(gated, wo_ref[...], preferred_element_type=f32)
+        out_ref[band, :] = (xbuf[band, :].astype(f32) + update).astype(bf16)
+
+        @pl.when(sec < sections - 1)
+        def _():
+            hop_fwd[index].start()
+
+    for move in to_chan + to_tok:
+        left(move)
+
     partner = me + 1 - 2 * lax.rem(me, 2)
     chips = parts // 2
     far, near = [], []
@@ -556,9 +602,11 @@
                 )
             )
 
-    def gather():
+    def gather_start():
         start(slope_move)
         start(far)
+
+    def gather_finish():
         for index in range(2):
             near[index * chips].start()
             for step in range(1, chips):
@@ -573,61 +621,74 @@
 
     early = sections // 2
 
+    @pl.when(sec < sections - 1)
+    def _():
+        gather_start()
+
+    @pl.when(sec == 0)
+    def _():
+        transpose_weights()
+
     @pl.when(sec < early)
     def _():
-        gather()
+        gather_finish()
 
     @pl.when(sec == sections - 1)
     def _():
         gbuf[...] = cot_ref[...]
 
-    @pl.when(sec < sections - 1)
-    def _():
-        hop_bwd.wait_recv()
-
-    contract_last = (((1,), (1,)), ((), ()))
-    contract_first = (((0,), (0,)), ((), ()))
-    dgated = lax.dot_general(gbuf[...], wo_ref[...], contract_last, preferred_element_type=f32)
-    send_b[...] = (dgated * gate_act[...].astype(f32)).astype(bf16)
-    grad_chan = exchange(3, col_block(send_b), row_block(chan_b, rows))
-    start(grad_chan)
-    dpre_gate = (dgated * mix_tok[...].astype(f32) * gate_slope[...]).astype(bf16)
-    dgate_send[...] = dpre_gate
-    dnormed_gate = lax.dot_general(
-        dpre_gate, wi_ref[:, :width], contract_last, preferred_element_type=f32
-    )
-    arrive(grad_chan)
-    arr_move = exchange(4, col_block(gbuf), row_block(arr_chan, rows))
-    dgate_move = exchange(5, col_block(dgate_send), row_block(dgate_chan, rows))
+    for index, band in enumerate(bands):
+
+        @pl.when(sec < sections - 1)
+        def _():
+            hop_bwd[index].wait_recv()
+
+        dgated = jnp.dot(gbuf[band, :], wo_t[...], preferred_element_type=f32)
+        send_b[band, :] = (dgated * gate_act[band, :].astype(f32)).astype(bf16)
+        start(grad_chan[index])
+        dgate_send[band, :] = (dgated * mix_tok[band, :].astype(f32) * gate_slope[band, :]).astype(
+            bf16
+        )
+    dnormed_gate[...] = jnp.dot(dgate_send[...], wi_t[:width, :], preferred_element_type=f32)
+    for move in grad_chan:
+        arrive(move)
     mix(chan_b, dval_chan, -1.0)
-    grad_tok = exchange(6, row_block(dval_chan, rows), col_block(dval_tok))
-    start(grad_tok)
+    for move in grad_tok:
+        start(move)
+
+    def result(part, lhs, rhs):
+        piece = lax.dot_general(
+            lhs, rhs[...], (((0,), (0,)), ((), ())), preferred_element_type=f32
+        )
+        res_send[part] = piece.astype(bf16)
+
+    for index, band in enumerate(bands):
+        arrive(grad_tok[index])
+        dpre_val = (dval_tok[band, :].astype(f32) * val_slope[band, :].astype(f32)).astype(bf16)
+        dnormed = dnormed_gate[band, :] + jnp.dot(
+            dpre_val, wi_t[width:, :], preferred_element_type=f32
+        )
+        dscaled = dnormed * gain
+        x_hat, inv_rms = scaled(band)
+        shared = jnp.mean(dscaled * x_hat, axis=1, keepdims=True)
+        gin_ref[band, :] = (
+            gbuf[band, :].astype(f32) + inv_rms * (dscaled - x_hat * shared)
+        ).astype(bf16)
+
+        @pl.when(sec > 0)
+        def _():
+            hop_bwd[index].start()
+
     start(arr_move)
     start(dgate_move)
 
-    def result(part, lhs, rhs):
-        piece = lax.dot_general(lhs, rhs[...], contract_first, preferred_element_type=f32)
-        res_send[part] = piece.astype(bf16)
-
-    arrive(grad_tok)
-    dpre_val = (dval_tok[...].astype(f32) * val_slope[...].astype(f32)).astype(bf16)
-    dnormed = dnormed_gate + lax.dot_general(
-        dpre_val, wi_ref[:, width:], contract_last, preferred_element_type=f32
-    )
-    x_float = xbuf[...].astype(f32)
-    inv_rms = lax.rsqrt(jnp.mean(x_float * x_float, axis=1, keepdims=True) + EPSILON)
-    dscaled = dnormed * gain
-    x_hat = x_float * inv_rms
-    shared = jnp.mean(dscaled * x_hat, axis=1, keepdims=True)
-    gin_ref[...] = (gbuf[...].astype(f32) + inv_rms * (dscaled - x_hat * shared)).astype(bf16)
-
-    @pl.when(sec > 0)
+    @pl.when(sec == sections - 1)
     def _():
-        hop_bwd.start()
+        gather_start()
 
     @pl.when(sec >= early)
     def _():
-        gather()
+        gather_finish()
 
     moves = []
     for part in range(3):
@@ -641,7 +702,7 @@
             arrive(dgate_move)
             result(2, dgate_chan[...], normed_all)
         move = exchange(
-            7 + part,
+            extra + 3 + part,
             lambda device, part=part: res_send.at[part, :, ds(device, cols)],
             lambda device, part=part: res_ref.at[part, ds(device, cols), :],
         )
@@ -650,16 +711,18 @@
     for move in moves:
         arrive(move)
         left(move)
-    for move in (grad_chan, grad_tok, arr_move, dgate_move):
+    for move in grad_chan + grad_tok + [arr_move, dgate_move]:
         left(move)
 
-    @pl.when(sec < sections - 1)
-    def _():
-        hop_fwd.wait_send()
-
-    @pl.when(sec > 0)
-    def _():
-        hop_bwd.wait_send()
+    for index in range(splits):
+
+        @pl.when(sec < sections - 1)
+        def _():
+            hop_fwd[index].wait_send()
+
+        @pl.when(sec > 0)
+        def _():
+            hop_bwd[index].wait_send()
 
 
 def on_device(
@@ -675,16 +738,16 @@
             tokens, cotangent, norm_gain, w_inner, w_outer, rpe_periods, rpe_in, rpe_mid, rpe_out, decay
         )
     bf16, f32 = jnp.bfloat16, jnp.float32
-    analysis = lax.optimization_barrier(dense_tables(length))
-    synthesis = analysis.T
+    splits = SPLITS
+    cos, sin, parity = dense_tables(length)
     kernel = kernel_rows(rpe_periods[0], rpe_in[0], rpe_mid[0], rpe_out[0], decay[0], length)
-    spec = lax.dot_general(
-        analysis, kernel.astype(bf16), (((1,), (1,)), ((), ())), preferred_element_type=f32
+    kernel = kernel.T.astype(bf16)
+    real, imag, nyquist = (
+        jnp.dot(table, kernel, preferred_element_type=f32) for table in (cos, sin, parity)
     )
     first = lax.broadcasted_iota(jnp.int32, (length, 1), 0) == 0
     scale = jnp.where(first, 0.5, 1.0) / length
-    real, imag = spec[:length] * scale, spec[length:] * scale
-    spec = jnp.stack([real, jnp.where(first, 0.0, imag), jnp.where(first, imag, real)])
+    spec = jnp.stack([real, imag, jnp.where(first, nyquist[:1], real)]) * scale
     tok_block = lambda kind: pltpu.VMEM((rows, width), kind)
     chan_block = lambda kind: pltpu.VMEM((length, cols), kind)
     vmem = pl.BlockSpec(memory_space=pltpu.VMEM)
@@ -696,7 +759,7 @@
             jax.ShapeDtypeStruct((rows, width), bf16),
             jax.ShapeDtypeStruct((3, width, cols), bf16),
         ),
-        in_specs=[vmem] * 8,
+        in_specs=[vmem] * 9,
         out_specs=(vmem,) * 3,
         scratch_shapes=[
             tok_block(bf16),
@@ -720,15 +783,18 @@
             pltpu.VMEM((length, width), bf16),
             pltpu.VMEM((length, width), bf16),
             pltpu.VMEM((3, cols, width), bf16),
-            dma((10, parts)),
-            dma((10, parts)),
-            dma((10,)),
+            pltpu.VMEM((width, width), bf16),
+            pltpu.VMEM((2 * width, width), bf16),
+            tok_block(f32),
+            dma((4 * splits + 6, parts)),
+            dma((4 * splits + 6, parts)),
+            dma((4 * splits + 6,)),
             dma((2, parts // 2)),
             dma((2, parts // 2)),
             dma((2, parts // 2)),
             dma((2, parts // 2)),
-            dma((2,)),
-            dma((2,)),
+            dma((2, splits)),
+            dma((2, splits)),
         ],
         compiler_params=pltpu.CompilerParams(
             collective_id=0, has_side_effects=True, vmem_limit_bytes=60 * 1024 * 1024
@@ -739,8 +805,9 @@
         norm_gain,
         w_inner[0],
         w_outer[0],
-        analysis,
-        synthesis,
+        cos,
+        sin,
+        parity,
         spec,
     )
     grad_scale = 1.0 / math.sqrt(length)

time: 267 us -> 232 us (0.87)
  Pallas kernels: 230 us -> 214 us
  local copies, waits for them, and re-layouts: 16.7 us -> 6.28 us
  other arithmetic: 13.2 us -> 5.51 us
    pallas_call x1, Pallas kernels: 230 us -> 214 us  [on_device(): pl.pallas_call(functools.partial(relay_kernel, parts, sections), out_shap...]
    optimization_barrier x1 -> x0, local copies, waits for them, and re-layouts: 6.41 us -> none  [on_device(): analysis = lax.optimization_barrier(dense_tables(length))]
    another operation x4 -> x1, other arithmetic: 5.54 us -> 0.21 us  [on_device(): spec = jnp.stack([real, imag, jnp.where(first, nyquist[:1], real)]) * scale]
    concatenate x1 -> x0, other arithmetic: 2.73 us -> none  [build(): return jnp.concatenate([cos, sin], axis=freq_axis).astype(jnp.bfloat16)]
where the time goes in v2:
time: 232 us; the launch traced here: 231 us
  Pallas kernels  214 us (92%)
  local copies, waits for them, and re-layouts  6.28 us (3%)
  other arithmetic  5.51 us (2%)
  matrix products  5.2 us (2%)
    pallas_call x1, Pallas kernels, on_device(): pl.pallas_call(functools.partial(relay_kernel, parts, sections), out_shap...  214 us

profile of v2, /device:TPU:1, one launch (start us, length us, event | category | flops | bytes accessed | tf_op | source)
XLA Modules:
  0.0 231.4 jit_solution(1603321391925442136)
XLA Ops:
  0.6 0.0 copy-start
  0.6 0.0 copy-start.5
  0.7 0.0 copy-start.6
  0.7 0.0 copy-start.7
  0.7 0.0 copy-start.8
  0.7 0.0 copy-start.10
  0.7 1.3 fusion.12
  2.1 1.8 convolution_maximum_fusion
  3.8 1.3 convolution_maximum_fusion.1
  5.1 0.0 copy-done.10
  5.2 0.0 copy-done
  5.2 0.6 fusion.1
  5.8 1.5 negate_convert_fusion
  7.3 0.0 copy-start.9
  7.3 0.7 fusion.17
  8.0 0.0 copy-done.9
  8.1 0.1 convolution_bitcast_fusion.1
  8.2 0.2 select_bitcast_fusion
  8.4 0.2 copy-done.2
  8.6 0.6 copy-done.1
  9.3 0.7 convolution_bitcast_fusion
  10.0 1.4 maximum_multiply_fusion.spec_ref
  11.4 0.6 broadcast.72.par_ref
  12.0 213.6 %shard_map.174 = (bf16[128,1024]{1,0:T(8,128)(2,1)}, bf16[128,1024]{1,0:T(8,128)(2,1)}, bf16[3,1024,128]{2,1,0:T(8,128)(2,1)}) custom-call(bf16[128,1024]{1,0:T(8,128)(2,1)} %tok_ref.1, bf16[128,1024]{1,0:T(8,128)(2,1)} %cot_ref.1, f32[1,1024]{1,0:T(1,128)} %gain_ref.1, bf16[1024,2048]{1,0:T(8,128)(2,1)} %bitcast.54, bf16[1024,1024]{1,0:T(8,128)(2,1)} %bitcast.55, ...), custom_call_target="tpu_custom_call" | custom-call | tf_op jit(solution)/shard_map/pallas_call | solution.py:755
  225.6 1.1 slice_bitcast_fusion.1
  226.6 0.1 multiply_bitcast_fusion
  226.7 1.3 copy.19
  228.0 1.0 multiply_bitcast_fusion.1
  229.0 1.0 copy.20
  230.0 0.0 copy-done.4
  230.0 0.7 copy.23
  230.7 0.7 copy.24
  (14 shorter events, 0.0 us)
Async XLA Ops:
  0.6 4.6 %copy-start = (f32[1,64,128]{2,1,0:T(8,128)S(1)}, f32[1,64,128]{2,1,0:T(8,128)}, u32[]{:S(2)}) copy-start(f32[1,64,128]{2,1,0:T(8,128)} %param.23) | copy-start | bytes 98308
  0.6 5.1 %copy-start.5 = (f32[32,1024]{1,0:T(8,128)S(1)}, f32[32,1024]{1,0:T(8,128)}, u32[]{:S(2)}) copy-start(f32[32,1024]{1,0:T(8,128)} %constant.45.clone) | copy-start | bytes 393220
  0.7 5.1 %copy-start.6 = (f32[32,1024]{1,0:T(8,128)S(1)}, f32[32,1024]{1,0:T(8,128)}, u32[]{:S(2)}) copy-start(f32[32,1024]{1,0:T(8,128)} %constant.46.clone) | copy-start | bytes 393220
  0.7 5.1 %copy-start.7 = (f32[32,1024]{1,0:T(8,128)S(1)}, f32[32,1024]{1,0:T(8,128)}, u32[]{:S(2)}) copy-start(f32[32,1024]{1,0:T(8,128)} %constant.47.clone) | copy-start | bytes 393220
  0.7 5.1 %copy-start.8 = (f32[32,1024]{1,0:T(8,128)S(1)}, f32[32,1024]{1,0:T(8,128)}, u32[]{:S(2)}) copy-start(f32[32,1024]{1,0:T(8,128)} %constant.48.clone) | copy-start | bytes 393220
  0.7 4.5 %copy-start.10 = (f32[1,128]{1,0:T(1,128)S(1)}, f32[1,128]{1,0:T(1,128)}, u32[]{:S(2)}) copy-start(f32[1,128]{1,0:T(1,128)} %param.24) | copy-start | bytes 1540
  7.3 1.3 copy-start.2
  7.3 1.9 copy-start.1
  7.3 0.7 copy-start.9
  226.7 3.3 %copy-start.4 = (bf16[128,1024]{1,0:T(8,128)(2,1)S(1)}, bf16[128,1024]{1,0:T(8,128)(2,1)}, u32[]{:S(2)}) copy-start(bf16[128,1024]{1,0:T(8,128)(2,1)} %get-tuple-element.7) | copy-start | bytes 786436
  226.7 4.0 %copy-start.3 = (bf16[128,1024]{1,0:T(8,128)(2,1)S(1)}, bf16[128,1024]{1,0:T(8,128)(2,1)}, u32[]{:S(2)}) copy-start(bf16[128,1024]{1,0:T(8,128)(2,1)} %get-tuple-element.8) | copy-start | bytes 786436

commit v3 on v2

--- a/solution.py
+++ b/solution.py
@@ -19,14 +19,14 @@
     return lax.ppermute(value, axis, [(source, source + steps) for source in range(initial, last)])
 
 
-def kernel_rows(periods, weight_in, weight_mid, weight_out, decay_rate, seq_length):
+def kernel_rows(periods, weight_in, weight_mid, weight_out, decay_rate, seq_length, precise=PRECISE):
     positions = jnp.arange(seq_length, dtype=jnp.int32)
     turn_count = periods[:, None] * positions[None, :] % seq_length
     angles = turn_count.astype(jnp.float32) * (2.0 * math.pi / seq_length)
     features = jnp.concatenate([jnp.sin(angles), jnp.cos(angles)], axis=0)
-    hidden = jax.nn.relu(jnp.dot(weight_in.T, features, precision=PRECISE))
-    hidden = jax.nn.relu(jnp.dot(weight_mid.T, hidden, precision=PRECISE))
-    raw_rows = jnp.dot(weight_out.T, hidden, precision=PRECISE)
+    hidden = jax.nn.relu(jnp.dot(weight_in.T, features, precision=precise))
+    hidden = jax.nn.relu(jnp.dot(weight_mid.T, hidden, precision=precise))
+    raw_rows = jnp.dot(weight_out.T, hidden, precision=precise)
     place = positions.astype(jnp.float32)
     norm_scale = jnp.sqrt(1.0 - jnp.exp(-2.0 * decay_rate))
     return raw_rows * norm_scale[:, None] * jnp.exp(-decay_rate[:, None] * place[None, :])
@@ -311,7 +311,7 @@
     )
 
 
-SPLITS = 2
+SPLITS = 4
 
 
 def dense_tables(seq_length):
@@ -649,6 +649,12 @@
         dgate_send[band, :] = (dgated * mix_tok[band, :].astype(f32) * gate_slope[band, :]).astype(
             bf16
         )
+
+    @pl.when(sec == 0)
+    def _():
+        start(arr_move)
+        start(dgate_move)
+
     dnormed_gate[...] = jnp.dot(dgate_send[...], wi_t[:width, :], preferred_element_type=f32)
     for move in grad_chan:
         arrive(move)
@@ -662,6 +668,30 @@
         )
         res_send[part] = piece.astype(bf16)
 
+    moves = [
+        exchange(
+            extra + 3 + part,
+            lambda device, part=part: res_send.at[part, :, ds(device, cols)],
+            lambda device, part=part: res_ref.at[part, ds(device, cols), :],
+        )
+        for part in range(3)
+    ]
+
+    def weight_grads():
+        dval = (dval_chan[...].astype(f32) * slope_chan[...].astype(f32)).astype(bf16)
+        result(0, dval, normed_all)
+        start(moves[0])
+        arrive(arr_move)
+        result(1, arr_chan[...], gated_all)
+        start(moves[1])
+        arrive(dgate_move)
+        result(2, dgate_chan[...], normed_all)
+        start(moves[2])
+
+    @pl.when(sec == 0)
+    def _():
+        weight_grads()
+
     for index, band in enumerate(bands):
         arrive(grad_tok[index])
         dpre_val = (dval_tok[band, :].astype(f32) * val_slope[band, :].astype(f32)).astype(bf16)
@@ -679,8 +709,10 @@
         def _():
             hop_bwd[index].start()
 
-    start(arr_move)
-    start(dgate_move)
+    @pl.when(sec > 0)
+    def _():
+        start(arr_move)
+        start(dgate_move)
 
     @pl.when(sec == sections - 1)
     def _():
@@ -690,24 +722,10 @@
     def _():
         gather_finish()
 
-    moves = []
-    for part in range(3):
-        if part == 0:
-            dval = (dval_chan[...].astype(f32) * slope_chan[...].astype(f32)).astype(bf16)
-            result(0, dval, normed_all)
-        elif part == 1:
-            arrive(arr_move)
-            result(1, arr_chan[...], gated_all)
-        else:
-            arrive(dgate_move)
-            result(2, dgate_chan[...], normed_all)
-        move = exchange(
-            extra + 3 + part,
-            lambda device, part=part: res_send.at[part, :, ds(device, cols)],
-            lambda device, part=part: res_ref.at[part, ds(device, cols), :],
-        )
-        start(move)
-        moves.append(move)
+    @pl.when(sec > 0)
+    def _():
+        weight_grads()
+
     for move in moves:
         arrive(move)
         left(move)
@@ -740,7 +758,7 @@
     bf16, f32 = jnp.bfloat16, jnp.float32
     splits = SPLITS
     cos, sin, parity = dense_tables(length)
-    kernel = kernel_rows(rpe_periods[0], rpe_in[0], rpe_mid[0], rpe_out[0], decay[0], length)
+    kernel = kernel_rows(rpe_periods[0], rpe_in[0], rpe_mid[0], rpe_out[0], decay[0], length, lax.Precision.HIGH)
     kernel = kernel.T.astype(bf16)
     real, imag, nyquist = (
         jnp.dot(table, kernel, preferred_element_type=f32) for table in (cos, sin, parity)

time: 232 us -> 220 us (0.948)
  Pallas kernels: 214 us -> 203 us
    pallas_call x1, Pallas kernels: 214 us -> 203 us  [on_device(): pl.pallas_call(functools.partial(relay_kernel, parts, sections), out_shap...]
where the time goes in v3:
time: 220 us
  Pallas kernels  203 us (92%)
  local copies, waits for them, and re-layouts  6.28 us (3%)
  other arithmetic  5.51 us (3%)
  matrix products  4.39 us (2%)
    pallas_call x1, Pallas kernels, on_device(): pl.pallas_call(functools.partial(relay_kernel, parts, sections), out_shap...  203 us
    unnamed x26, local copies, waits for them, and re-layouts  4.59 us

profile of v3, /device:TPU:1, one launch (start us, length us, event | category | flops | bytes accessed | tf_op | source)
XLA Modules:
  0.0 219.7 jit_solution(3798518599655111957)
XLA Ops:
  0.6 0.0 copy-start
  0.6 0.0 copy-start.5
  0.7 0.0 copy-start.6
  0.7 0.0 copy-start.7
  0.7 0.0 copy-start.8
  0.7 1.3 fusion.12
  2.1 1.4 convolution_maximum_fusion
  3.4 1.1 convolution_maximum_fusion.1
  4.5 0.0 copy-done.10
  4.6 0.0 copy-done
  4.6 0.4 fusion.1
  5.0 0.0 copy-done.5
  5.0 0.0 copy-done.6
  5.0 1.5 negate_convert_fusion
  6.5 0.0 copy-start.9
  6.5 0.7 fusion.17
  7.2 0.0 copy-done.9
  7.3 0.1 convolution_bitcast_fusion.1
  7.4 0.2 select_bitcast_fusion
  7.6 0.2 copy-done.2
  7.8 0.6 copy-done.1
  8.4 0.7 convolution_bitcast_fusion
  9.2 1.4 maximum_multiply_fusion.spec_ref
  10.6 0.6 broadcast.72.par_ref
  11.2 202.6 %shard_map.174 = (bf16[128,1024]{1,0:T(8,128)(2,1)}, bf16[128,1024]{1,0:T(8,128)(2,1)}, bf16[3,1024,128]{2,1,0:T(8,128)(2,1)}) custom-call(bf16[128,1024]{1,0:T(8,128)(2,1)} %tok_ref.1, bf16[128,1024]{1,0:T(8,128)(2,1)} %cot_ref.1, f32[1,1024]{1,0:T(1,128)} %gain_ref.1, bf16[1024,2048]{1,0:T(8,128)(2,1)} %bitcast.54, bf16[1024,1024]{1,0:T(8,128)(2,1)} %bitcast.55, ...), custom_call_target="tpu_custom_call" | custom-call | tf_op jit(solution)/shard_map/pallas_call | solution.py:773
  213.8 1.1 slice_bitcast_fusion.1
  214.9 0.1 multiply_bitcast_fusion
  215.0 1.3 copy.19
  216.3 1.0 multiply_bitcast_fusion.1
  217.3 1.0 copy.20
  218.3 0.7 copy.23
  219.0 0.7 copy.24
  (14 shorter events, 0.0 us)
Async XLA Ops:
  0.6 3.9 %copy-start = (f32[1,64,128]{2,1,0:T(8,128)S(1)}, f32[1,64,128]{2,1,0:T(8,128)}, u32[]{:S(2)}) copy-start(f32[1,64,128]{2,1,0:T(8,128)} %param.23) | copy-start | bytes 98308
  0.6 4.3 %copy-start.5 = (f32[32,1024]{1,0:T(8,128)S(1)}, f32[32,1024]{1,0:T(8,128)}, u32[]{:S(2)}) copy-start(f32[32,1024]{1,0:T(8,128)} %constant.45.clone) | copy-start | bytes 393220
  0.7 4.3 %copy-start.6 = (f32[32,1024]{1,0:T(8,128)S(1)}, f32[32,1024]{1,0:T(8,128)}, u32[]{:S(2)}) copy-start(f32[32,1024]{1,0:T(8,128)} %constant.46.clone) | copy-start | bytes 393220
  0.7 4.3 %copy-start.7 = (f32[32,1024]{1,0:T(8,128)S(1)}, f32[32,1024]{1,0:T(8,128)}, u32[]{:S(2)}) copy-start(f32[32,1024]{1,0:T(8,128)} %constant.47.clone) | copy-start | bytes 393220
  0.7 4.3 %copy-start.8 = (f32[32,1024]{1,0:T(8,128)S(1)}, f32[32,1024]{1,0:T(8,128)}, u32[]{:S(2)}) copy-start(f32[32,1024]{1,0:T(8,128)} %constant.48.clone) | copy-start | bytes 393220
  0.7 3.8 %copy-start.10 = (f32[1,128]{1,0:T(1,128)S(1)}, f32[1,128]{1,0:T(1,128)}, u32[]{:S(2)}) copy-start(f32[1,128]{1,0:T(1,128)} %param.24) | copy-start | bytes 1540
  6.5 1.3 copy-start.2
  6.5 1.9 copy-start.1
  6.5 0.7 copy-start.9
  214.9 3.3 %copy-start.4 = (bf16[128,1024]{1,0:T(8,128)(2,1)S(1)}, bf16[128,1024]{1,0:T(8,128)(2,1)}, u32[]{:S(2)}) copy-start(bf16[128,1024]{1,0:T(8,128)(2,1)} %get-tuple-element.7) | copy-start | bytes 786436
  215.0 4.0 %copy-start.3 = (bf16[128,1024]{1,0:T(8,128)(2,1)S(1)}, bf16[128,1024]{1,0:T(8,128)(2,1)}, u32[]{:S(2)}) copy-start(bf16[128,1024]{1,0:T(8,128)(2,1)} %get-tuple-element.8) | copy-start | bytes 786436
